TPU v7x, 768 devices: a whole 4x8x12 slice. The times are simulated.
768 devices in a mesh: lat: 48 (over z, y_hi, core), lon: 16 (over x, y_lo).
Axes of the slice: x: 4, y: 8 (y_hi: 2, y_lo: 4; y = y_hi * 4 + y_lo), z: 12, core: 2. Of those that a mesh axis runs over, the one named last changes fastest.
Arguments:
- fields: bfloat16 [192, 1440, 256], P('lat', 'lon'), may hold values from -6 to 6
- w_mix: bfloat16 [256, 1024], replicated, may hold values from -0.375 to 0.375
- filters: bfloat16 [4, 192, 3, 17], P(None, 'lat'), may hold values from -0.5 to 0.5
- reach: int32 [192], P('lat'), may hold values from 1 to 8, as said below
- w_up: bfloat16 [256, 512], replicated, may hold values from -0.375 to 0.375
- w_down: bfloat16 [512, 256], replicated, may hold values from -0.25 to 0.25
- cotangent: bfloat16 [192, 1440, 256], P('lat', 'lon'), may hold values from -6 to 6
Outputs:
- result: bfloat16 [192, 1440, 256], P('lat', 'lon')
- field_grad: bfloat16 [192, 1440, 256], P('lat', 'lon')
Inputs may be any that keep to these rules, and one draw needn't show every extreme that they name: reach equals 8 at the two rows at each end of the grid.
All inputs are finite; a program needn't handle non-finite values.
Results may differ from a plain program's by a relative error of at most 0.0061.
Values may be sent and summed in bfloat16 or wider, within the bound.
A program may use at most 32 MiB of HBM per device.

v0:
```python
import jax
import jax.numpy as jnp
from jax import lax
from jax.sharding import PartitionSpec as P

KB = 4
LREACH = 8


def padded_2(cells, sides, width, closed):
    for axis, dim in sides:
        count = lax.axis_size(axis)
        ends = count if closed else count - 1
        head = lax.slice_in_dim(cells, 0, width, axis=dim)
        tail = lax.slice_in_dim(cells, cells.shape[dim] - width, cells.shape[dim], axis=dim)
        cells = jnp.concatenate(
            [
                lax.ppermute(tail, axis, [(i, (i + 1) % count) for i in range(ends)]),
                cells,
                lax.ppermute(head, axis, [((i + 1) % count, i) for i in range(ends)]),
            ],
            axis=dim,
        )
    return cells


def gelu_value(pre):
    return 0.5 * pre * (1.0 + jax.scipy.special.erf(pre * 0.7071067811865476))


def gelu_slope(pre):
    return (
        0.5 * (1.0 + jax.scipy.special.erf(pre * 0.7071067811865476))
        + pre * jnp.exp(-0.5 * pre * pre) * 0.3989422804014327
    )


def masked_filters(filters, reach):
    offsets = jnp.arange(2 * LREACH + 1, dtype=jnp.int32) - LREACH
    keep = (jnp.abs(offsets)[None, :] <= reach[:, None]).astype(filters.dtype)
    return filters * keep[None, :, None, :]


def band_table(width):
    shape = (width, width + 2 * LREACH, 2 * LREACH + 1)
    column = lax.broadcasted_iota(jnp.int32, shape, 0)
    extended = lax.broadcasted_iota(jnp.int32, shape, 1)
    offset = lax.broadcasted_iota(jnp.int32, shape, 2)
    return (extended - column == offset).astype(jnp.bfloat16)


def contract_last(left, right):
    return lax.dot_general(
        left, right, (((1,), (1,)), ((), ())), preferred_element_type=jnp.float32
    )


def spatial_sum(coeffs, mixed, rows, width, chans):
    span = width + 2 * LREACH
    total = jnp.zeros((rows, width, chans), jnp.float32)
    for lat_tap in range(3):
        source = mixed[lat_tap : lat_tap + rows].reshape(rows, span * KB, chans)
        total = total + jnp.einsum(
            "rjn,rnc->rjc", coeffs[:, lat_tap], source, preferred_element_type=jnp.float32
        )
    return total


def mlp_pass(hidden, upstream, w_up, w_down):
    flat_hidden = hidden.reshape(-1, hidden.shape[-1])
    pre = jnp.dot(flat_hidden, w_up, preferred_element_type=jnp.float32)
    active = gelu_value(pre).astype(jnp.bfloat16)
    result = (
        flat_hidden.astype(jnp.float32)
        + jnp.dot(active, w_down, preferred_element_type=jnp.float32)
    ).astype(jnp.bfloat16)
    flat_up = upstream.reshape(-1, upstream.shape[-1])
    grad_active = (contract_last(flat_up, w_down) * gelu_slope(pre)).astype(jnp.bfloat16)
    grad_hidden = (flat_up.astype(jnp.float32) + contract_last(grad_active, w_up)).astype(
        jnp.bfloat16
    )
    return (result.reshape(hidden.shape), grad_hidden.reshape(hidden.shape))


def on_device(fields, w_mix, filters, reach, w_up, w_down, cotangent):
    rows, width, chans = fields.shape
    span = width + 2 * LREACH
    masked = masked_filters(filters, reach)
    band = band_table(width)
    coeffs = jnp.einsum("jmb,krab->rajmk", band, masked, preferred_element_type=jnp.float32).astype(
        jnp.bfloat16
    )
    coeffs = coeffs.reshape(rows, 3, width, span * KB)
    padded = padded_2(fields, (("lat", 0),), 1, False)
    padded = padded_2(padded, (("lon", 1),), LREACH, True)
    mixed = jnp.dot(padded.reshape(-1, chans), w_mix, preferred_element_type=jnp.float32).astype(
        jnp.bfloat16
    )
    mixed = mixed.reshape(rows + 2, span, KB * chans)
    spatial = spatial_sum(coeffs, mixed, rows, width, chans)
    hidden = (fields.astype(jnp.float32) + spatial).astype(jnp.bfloat16)
    result, grad_grid = mlp_pass(hidden, cotangent, w_up, w_down)
    partial_sums = jnp.zeros((rows + 2, span * KB, chans), jnp.float32)
    for lat_tap in range(3):
        term = jnp.einsum(
            "rjn,rjc->rnc", coeffs[:, lat_tap], grad_grid, preferred_element_type=jnp.float32
        )
        partial_sums = partial_sums.at[lat_tap : lat_tap + rows].add(term)
    partial_sums = partial_sums.reshape(rows + 2, span, KB * chans)
    edges = jnp.stack([partial_sums[0], partial_sums[rows + 1]])
    arrived = padded_2(edges, (("lat", 0),), 1, False)
    inner = partial_sums[1 : rows + 1]
    inner = inner.at[0].add(arrived[0])
    inner = inner.at[rows - 1].add(arrived[3])
    sides = jnp.concatenate([inner[:, :LREACH], inner[:, width + LREACH :]], axis=1)
    incoming = padded_2(sides, (("lon", 1),), LREACH, True)
    core = inner[:, LREACH : LREACH + width]
    core = core.at[:, :LREACH].add(incoming[:, :LREACH])
    core = core.at[:, width - LREACH :].add(incoming[:, 3 * LREACH :])
    grad_mixed = core.astype(jnp.bfloat16)
    field_grad = grad_grid.reshape(-1, chans).astype(jnp.float32) + contract_last(
        grad_mixed.reshape(-1, KB * chans), w_mix
    )
    field_grad = field_grad.astype(jnp.bfloat16).reshape(rows, width, chans)
    return (result, field_grad)


def solution(mesh):
    return jax.shard_map(
        on_device,
        mesh=mesh,
        in_specs=(
            P("lat", "lon", None),
            P(),
            P(None, "lat", None, None),
            P("lat"),
            P(),
            P(),
            P("lat", "lon", None),
        ),
        out_specs=(P("lat", "lon", None), P("lat", "lon", None)),
        check_vma=False,
    )
```

profile of v0, /device:TPU:318, one launch (start us, length us, event | category | flops | bytes accessed | tf_op | source)
XLA Modules:
  0.0 102.8 jit_solution(15011654814811214241)
XLA Ops:
  0.7 1.3 %fusion.35 = (bf16[1,90,256]{2,0,1:T(2,128)(2,1)S(1)}, bf16[1,90,256]{2,0,1:T(2,128)(2,1)S(1)}) fusion(bf16[4,90,256]{2,0,1:T(4,128)(2,1)} %param.21), kind=kLoop, calls=%fused_computation.60 | loop fusion | bytes 184320 | tf_op jit(solution)/shard_map/slice | solution.py:15
  1.9 1.9 %collective-permute-start = (bf16[1,90,256]{2,0,1:T(2,128)(2,1)S(1)}, bf16[1,90,256]{2,0,1:T(2,128)(2,1)S(1)}, u32[]{:S(2)}, u32[]{:S(2)}) collective-permute-start(bf16[1,90,256]{2,0,1:T(2,128)(2,1)S(1)} %get-tuple-element.99), channel_id=1, source_target_pairs={{0,16},{16,32},{32,48},{48,64},{64,80},{80,96},{96,112},{112,128},... | collective-permute-start | bytes 138248 | tf_op jit(solution)/shard_map/ppermute | solution.py:18
  3.8 7.5 %collective-permute-start.1 = (bf16[1,90,256]{2,0,1:T(2,128)(2,1)S(1)}, bf16[1,90,256]{2,0,1:T(2,128)(2,1)S(1)}, u32[]{:S(2)}, u32[]{:S(2)}) collective-permute-start(bf16[1,90,256]{2,0,1:T(2,128)(2,1)S(1)} %get-tuple-element.100), channel_id=1, source_target_pairs={{16,0},{32,16},{48,32},{64,48},{80,64},{96,80},{112,96},{128,112},... | collective-permute-start | bytes 138248 | tf_op jit(solution)/shard_map/ppermute | solution.py:20
  12.1 1.4 %collective-permute-done.1 = bf16[1,90,256]{2,0,1:T(2,128)(2,1)S(1)} collective-permute-done((bf16[1,90,256]{2,0,1:T(2,128)(2,1)S(1)}, bf16[1,90,256]{2,0,1:T(2,128)(2,1)S(1)}, u32[]{:S(2)}, u32[]{:S(2)}) %collective-permute-start.1) | collective-permute-done | bytes 46112 | tf_op jit(solution)/shard_map/ppermute | solution.py:20
  14.3 4.7 %collective-permute-start.2 = (bf16[6,8,256]{2,0,1:T(8,128)(2,1)S(1)}, bf16[6,8,256]{2,0,1:T(8,128)(2,1)S(1)}, u32[]{:S(2)}, u32[]{:S(2)}) collective-permute-start(bf16[6,8,256]{2,0,1:T(8,128)(2,1)S(1)} %get-tuple-element.97), channel_id=1, source_target_pairs={{0,1},{1,2},{2,3},{3,4},{4,5},{5,6},{6,7},{7,8},{8,9},{9,10},{10,1... | collective-permute-start | bytes 73736 | tf_op jit(solution)/shard_map/ppermute | solution.py:18
  19.1 1.9 %collective-permute-start.3 = (bf16[6,8,256]{2,0,1:T(8,128)(2,1)S(1)}, bf16[6,8,256]{2,0,1:T(8,128)(2,1)S(1)}, u32[]{:S(2)}, u32[]{:S(2)}) collective-permute-start(bf16[6,8,256]{2,0,1:T(8,128)(2,1)S(1)} %get-tuple-element.98), channel_id=1, source_target_pairs={{1,0},{2,1},{3,2},{4,3},{5,4},{6,5},{7,6},{8,7},{9,8},{10,9},{11,1... | collective-permute-start | bytes 73736 | tf_op jit(solution)/shard_map/ppermute | solution.py:20
  21.0 1.2 %fusion = bf16[4,3,90,106,4]{3,0,2,1,4:T(4,128)(2,1)S(1)} fusion(bf16[4,4,3,17]{3,1,2,0:T(4,128)(2,1)} %param.23, bf16[4,17]{1,0:T(4,128)(2,1)S(1)} %compare_convert_fusion), kind=kOutput, calls=%fused_computation.4 | convolution fusion | flops 16354824 | bytes 917608 | tf_op jit(solution)/shard_map/jmb,krab->rajmk/dot_general | solution.py:90
  23.0 1.2 %copy.14 = bf16[4,3,90,106,4]{2,4,3,1,0:T(4,128)(2,1)S(1)} copy(bf16[4,3,90,106,4]{3,0,2,1,4:T(4,128)(2,1)S(1)} %fusion) | data formatting | bytes 1831680 | tf_op jit(solution)/shard_map/convert_element_type | solution.py:90
  24.2 4.6 %collective-permute-done.3 = bf16[6,8,256]{2,0,1:T(8,128)(2,1)S(1)} collective-permute-done((bf16[6,8,256]{2,0,1:T(8,128)(2,1)S(1)}, bf16[6,8,256]{2,0,1:T(8,128)(2,1)S(1)}, u32[]{:S(2)}, u32[]{:S(2)}) %collective-permute-start.3) | collective-permute-done | bytes 24608 | tf_op jit(solution)/shard_map/ppermute | solution.py:20
  29.8 1.6 %fusion.34 = (bf16[424,1024]{1,0:T(8,128)(2,1)}, bf16[424,1024]{1,0:T(8,128)(2,1)}, bf16[424,1024]{1,0:T(8,128)(2,1)S(1)}) fusion(bf16[636,1024]{1,0:T(8,128)(2,1)S(1)} %convolution_convert_fusion), kind=kLoop, calls=%fused_computation.59 | loop fusion | bytes 5210112 | tf_op jit(solution)/shard_map/slice | solution.py:62
  31.4 2.3 %reshape.287 = bf16[4,424,256]{2,1,0:T(8,128)(2,1)} reshape(bf16[424,1024]{1,0:T(8,128)(2,1)} %get-tuple-element.94) | data formatting | bytes 1736704 | tf_op jit(solution)/shard_map/reshape | solution.py:62
  33.8 2.3 %reshape.286 = bf16[4,424,256]{2,1,0:T(8,128)(2,1)} reshape(bf16[424,1024]{1,0:T(8,128)(2,1)} %get-tuple-element.95) | data formatting | bytes 1736704 | tf_op jit(solution)/shard_map/reshape | solution.py:62
  36.1 1.4 %reshape.285 = bf16[4,424,256]{2,1,0:T(8,128)(2,1)} reshape(bf16[424,1024]{1,0:T(8,128)(2,1)S(1)} %get-tuple-element.96) | data formatting | bytes 1736704 | tf_op jit(solution)/shard_map/reshape | solution.py:62
  37.5 1.6 %fusion.19 = f32[4,90,256]{2,1,0:T(8,128)S(1)} fusion(bf16[4,424,256]{2,1,0:T(8,128)(2,1)} %reshape.285, bf16[4,3,90,424]{2,3,1,0:T(8,128)(2,1)S(1)} %bitcast.49), kind=kOutput, calls=%fused_computation.36 | convolution fusion | flops 78151680 | bytes 1671168 | tf_op jit(solution)/shard_map/rjn,rnc->rjc/dot_general | solution.py:63
  40.8 2.0 %fusion.7 = bf16[360,256]{1,0:T(8,128)(2,1)S(1)} fusion(bf16[256,512]{1,0:T(8,128)(2,1)} %param.25, bf16[360,256]{1,0:T(8,128)(2,1)} %reshape.290, bf16[512,256]{1,0:T(8,128)(2,1)} %param.26, f32[360,512]{1,0:T(8,128)S(1)} %fusion.36), kind=kOutput, calls=%fused_computation.16 | convolution fusion | flops 190863360 | bytes 1630208 | tf_op jit(solution)/shard_map/dot_general | solution.py:53
  43.4 1.1 %copy-done.2 = bf16[4,3,90,106,4]{2,4,3,1,0:T(4,128)(2,1)S(1)} copy-done((bf16[4,3,90,106,4]{2,4,3,1,0:T(4,128)(2,1)S(1)}, bf16[4,3,90,106,4]{2,4,3,1,0:T(4,128)(2,1)}, u32[]{:S(2)}) %copy-start.2) | copy-done | bytes 915864
  46.4 1.9 %slice.244 = f32[1,106,1024]{2,1,0:T(8,128)} reshape(f32[1,424,256]{2,1,0:T(8,128)} %slice.262) | data formatting | bytes 868352 | tf_op jit(solution)/shard_map/slice | solution.py:110
  48.3 4.2 %collective-permute-start.4 = (f32[1,106,1024]{2,1,0:T(8,128)}, f32[1,106,1024]{2,1,0:T(8,128)}, u32[]{:S(2)}, u32[]{:S(2)}) collective-permute-start(f32[1,106,1024]{2,1,0:T(8,128)} %slice.244), channel_id=1, source_target_pairs={{0,16},{16,32},{32,48},{48,64},{64,80},{80,96},{96,112},{112,128},... | collective-permute-start | bytes 1302536 | tf_op jit(solution)/shard_map/ppermute | solution.py:18
  52.5 1.0 fusion.32
  53.5 1.9 %slice.247 = f32[1,106,1024]{2,1,0:T(8,128)} reshape(f32[1,424,256]{2,1,0:T(8,128)} %get-tuple-element.90) | data formatting | bytes 868352 | tf_op jit(solution)/shard_map/slice | solution.py:110
  55.4 5.2 %collective-permute-start.5 = (f32[1,106,1024]{2,1,0:T(8,128)}, f32[1,106,1024]{2,1,0:T(8,128)}, u32[]{:S(2)}, u32[]{:S(2)}) collective-permute-start(f32[1,106,1024]{2,1,0:T(8,128)} %slice.247), channel_id=1, source_target_pairs={{16,0},{32,16},{48,32},{64,48},{80,64},{96,80},{112,96},{128,112},... | collective-permute-start | bytes 1302536 | tf_op jit(solution)/shard_map/ppermute | solution.py:20
  60.6 1.4 %slice.260 = f32[4,424,256]{2,1,0:T(8,128)} slice(f32[6,424,256]{2,1,0:T(8,128)S(1)} %get-tuple-element.101), slice={[1:5], [0:424], [0:256]} | slice | bytes 3473408 | tf_op jit(solution)/shard_map/slice | solution.py:112
  62.0 1.9 %slice.241 = f32[4,106,1024]{2,1,0:T(8,128)S(1)} reshape(f32[4,424,256]{2,1,0:T(8,128)} %slice.260) | data formatting | bytes 3473408 | tf_op jit(solution)/shard_map/slice | solution.py:112
  64.1 14.0 %collective-permute-done.4 = f32[1,106,1024]{2,1,0:T(8,128)} collective-permute-done((f32[1,106,1024]{2,1,0:T(8,128)}, f32[1,106,1024]{2,1,0:T(8,128)}, u32[]{:S(2)}, u32[]{:S(2)}) %collective-permute-start.4) | collective-permute-done | bytes 434208 | tf_op jit(solution)/shard_map/ppermute | solution.py:18
  78.1 1.1 %add_dynamic-update-slice_fusion.1 = f32[4,106,1024]{2,1,0:T(8,128)S(1)} fusion(f32[4,106,1024]{2,1,0:T(8,128)S(1)} %slice.241, f32[1,106,1024]{2,1,0:T(8,128)S(1)} %reshape.292, f32[1,106,1024]{2,1,0:T(8,128)} %collective-permute-done.4), kind=kLoop, calls=%fused_computation.30 | loop fusion | flops 108544 | bytes 1351680 | tf_op jit(solution)/shard_map/scatter-add | solution.py:113
  79.1 1.1 %fusion.17 = f32[4,106,1024]{2,1,0:T(8,128)S(1)} fusion(f32[4,106,1024]{2,1,0:T(8,128)S(1)} %add_dynamic-update-slice_fusion.1, f32[1,106,1024]{2,1,0:T(8,128)} %collective-permute-done.5), kind=kLoop, calls=%fused_computation.29 | loop fusion | flops 108544 | bytes 1351680 | tf_op jit(solution)/shard_map/scatter-add | solution.py:114
  81.0 4.9 %collective-permute-start.6 = (f32[4,8,1024]{2,1,0:T(8,128)}, f32[4,8,1024]{2,1,0:T(8,128)S(1)}, u32[]{:S(2)}, u32[]{:S(2)}) collective-permute-start(f32[4,8,1024]{2,1,0:T(8,128)} %get-tuple-element.93), channel_id=1, source_target_pairs={{0,1},{1,2},{2,3},{3,4},{4,5},{5,6},{6,7},{7,8},{8,9},{9,10},{10,1... | collective-permute-start | bytes 393224 | tf_op jit(solution)/shard_map/ppermute | solution.py:18
  86.3 0.8 copy.20
  87.3 1.9 %collective-permute-start.7 = (f32[4,8,1024]{2,1,0:T(8,128)S(1)}, f32[4,8,1024]{2,1,0:T(8,128)S(1)}, u32[]{:S(2)}, u32[]{:S(2)}) collective-permute-start(f32[4,8,1024]{2,1,0:T(8,128)S(1)} %copy-done.14), channel_id=1, source_target_pairs={{1,0},{2,1},{3,2},{4,3},{5,4},{6,5},{7,6},{8,7},{9,8},{10,9},{11,1... | collective-permute-start | bytes 393224 | tf_op jit(solution)/shard_map/ppermute | solution.py:20
  89.3 8.8 %collective-permute-done.7 = f32[4,8,1024]{2,1,0:T(8,128)S(1)} collective-permute-done((f32[4,8,1024]{2,1,0:T(8,128)S(1)}, f32[4,8,1024]{2,1,0:T(8,128)S(1)}, u32[]{:S(2)}, u32[]{:S(2)}) %collective-permute-start.7) | collective-permute-done | bytes 131104 | tf_op jit(solution)/shard_map/ppermute | solution.py:20
  98.1 1.7 %scatter-add.34 = f32[4,90,1024]{2,1,0:T(8,128)} dynamic-update-slice(f32[4,90,1024]{2,1,0:T(8,128)} %copy-done.3, f32[4,8,1024]{2,1,0:T(8,128)S(1)} %slice_add_fusion.2, s32[]{:T(128)} %constant.197.clone.1, s32[]{:T(128)} %constant.200.clone.1, s32[]{:T(128)} %constant.197.clone.1) | dynamic-update-slice | bytes 262148 | tf_op jit(solution)/shard_map/scatter-add | solution.py:119
  99.8 1.5 %convert_element_type.63 = bf16[4,90,1024]{2,1,0:T(8,128)(2,1)S(1)} convert(f32[4,90,1024]{2,1,0:T(8,128)} %scatter-add.34) | non-fusion elementwise | flops 368640 | bytes 2211840 | tf_op jit(solution)/shard_map/convert_element_type | solution.py:120
  (65 shorter events, 10.2 us)
Async XLA Ops:
  0.6 28.7 %copy-start = (bf16[256,1024]{1,0:T(8,128)(2,1)S(1)}, bf16[256,1024]{1,0:T(8,128)(2,1)}, u32[]{:S(2)}) copy-start(bf16[256,1024]{1,0:T(8,128)(2,1)} %param.22) | copy-start | bytes 1572868
  0.6 21.6 %copy-start.13 = (bf16[4,90,256]{2,0,1:T(4,128)(2,1)S(1)}, bf16[4,90,256]{2,0,1:T(4,128)(2,1)}, u32[]{:S(2)}) copy-start(bf16[4,90,256]{2,0,1:T(4,128)(2,1)} %param.27) | copy-start | bytes 552964
  1.9 10.2 %collective-permute-start = (bf16[1,90,256]{2,0,1:T(2,128)(2,1)S(1)}, bf16[1,90,256]{2,0,1:T(2,128)(2,1)S(1)}, u32[]{:S(2)}, u32[]{:S(2)}) collective-permute-start(bf16[1,90,256]{2,0,1:T(2,128)(2,1)S(1)} %get-tuple-element.99), channel_id=1, source_target_pairs={{0,16},{16,32},{32,48},{48,64},{64,80},{80,96},{96,112},{112,128},... | collective-permute-start | bytes 138248 | tf_op jit(solution)/shard_map/ppermute | solution.py:18
  3.8 9.7 %collective-permute-start.1 = (bf16[1,90,256]{2,0,1:T(2,128)(2,1)S(1)}, bf16[1,90,256]{2,0,1:T(2,128)(2,1)S(1)}, u32[]{:S(2)}, u32[]{:S(2)}) collective-permute-start(bf16[1,90,256]{2,0,1:T(2,128)(2,1)S(1)} %get-tuple-element.100), channel_id=1, source_target_pairs={{16,0},{32,16},{48,32},{64,48},{80,64},{96,80},{112,96},{128,112},... | collective-permute-start | bytes 138248 | tf_op jit(solution)/shard_map/ppermute | solution.py:20
  14.3 9.9 %collective-permute-start.2 = (bf16[6,8,256]{2,0,1:T(8,128)(2,1)S(1)}, bf16[6,8,256]{2,0,1:T(8,128)(2,1)S(1)}, u32[]{:S(2)}, u32[]{:S(2)}) collective-permute-start(bf16[6,8,256]{2,0,1:T(8,128)(2,1)S(1)} %get-tuple-element.97), channel_id=1, source_target_pairs={{0,1},{1,2},{2,3},{3,4},{4,5},{5,6},{6,7},{7,8},{8,9},{9,10},{10,1... | collective-permute-start | bytes 73736 | tf_op jit(solution)/shard_map/ppermute | solution.py:18
  19.1 9.7 %collective-permute-start.3 = (bf16[6,8,256]{2,0,1:T(8,128)(2,1)S(1)}, bf16[6,8,256]{2,0,1:T(8,128)(2,1)S(1)}, u32[]{:S(2)}, u32[]{:S(2)}) collective-permute-start(bf16[6,8,256]{2,0,1:T(8,128)(2,1)S(1)} %get-tuple-element.98), channel_id=1, source_target_pairs={{1,0},{2,1},{3,2},{4,3},{5,4},{6,5},{7,6},{8,7},{9,8},{10,9},{11,1... | collective-permute-start | bytes 73736 | tf_op jit(solution)/shard_map/ppermute | solution.py:20
  22.2 6.6 %copy-start.6 = (bf16[4,90,256]{2,0,1:T(4,128)(2,1)S(1)}, bf16[4,90,256]{2,0,1:T(4,128)(2,1)}, u32[]{:S(2)}) copy-start(bf16[4,90,256]{2,0,1:T(4,128)(2,1)} %param.21) | copy-start | bytes 552964
  24.2 18.6 %copy-start.1 = (bf16[4,3,90,106,4]{2,4,3,1,0:T(4,128)(2,1)}, bf16[4,3,90,106,4]{2,4,3,1,0:T(4,128)(2,1)S(1)}, u32[]{:S(2)}) copy-start(bf16[4,3,90,106,4]{2,4,3,1,0:T(4,128)(2,1)S(1)} %copy.14) | copy-start | bytes 2747524
  37.5 1.7 %copy-start.5 = (bf16[4,424,256]{2,1,0:T(8,128)(2,1)S(1)}, bf16[4,424,256]{2,1,0:T(8,128)(2,1)}, u32[]{:S(2)}) copy-start(bf16[4,424,256]{2,1,0:T(8,128)(2,1)} %reshape.286) | copy-start | bytes 2605060
  37.5 2.0 %copy-start.4 = (bf16[4,424,256]{2,1,0:T(8,128)(2,1)S(1)}, bf16[4,424,256]{2,1,0:T(8,128)(2,1)}, u32[]{:S(2)}) copy-start(bf16[4,424,256]{2,1,0:T(8,128)(2,1)} %reshape.287) | copy-start | bytes 2605060
  39.6 1.0 copy-start.12
  40.5 2.2 %copy-start.8 = (bf16[360,256]{1,0:T(8,128)(2,1)}, bf16[360,256]{1,0:T(8,128)(2,1)S(1)}, u32[]{:S(2)}) copy-start(bf16[360,256]{1,0:T(8,128)(2,1)S(1)} %reshape.288) | copy-start | bytes 552964
  40.8 2.1 %copy-start.10 = (f32[360,512]{1,0:T(8,128)}, f32[360,512]{1,0:T(8,128)S(1)}, u32[]{:S(2)}) copy-start(f32[360,512]{1,0:T(8,128)S(1)} %fusion.36) | copy-start | bytes 2211844
  43.2 1.3 %copy-start.2 = (bf16[4,3,90,106,4]{2,4,3,1,0:T(4,128)(2,1)S(1)}, bf16[4,3,90,106,4]{2,4,3,1,0:T(4,128)(2,1)}, u32[]{:S(2)}) copy-start(bf16[4,3,90,106,4]{2,4,3,1,0:T(4,128)(2,1)} %copy-done.1) | copy-start | bytes 2747524
  48.3 29.8 %collective-permute-start.4 = (f32[1,106,1024]{2,1,0:T(8,128)}, f32[1,106,1024]{2,1,0:T(8,128)}, u32[]{:S(2)}, u32[]{:S(2)}) collective-permute-start(f32[1,106,1024]{2,1,0:T(8,128)} %slice.244), channel_id=1, source_target_pairs={{0,16},{16,32},{32,48},{48,64},{64,80},{80,96},{96,112},{112,128},... | collective-permute-start | bytes 1302536 | tf_op jit(solution)/shard_map/ppermute | solution.py:18
  55.4 23.7 %collective-permute-start.5 = (f32[1,106,1024]{2,1,0:T(8,128)}, f32[1,106,1024]{2,1,0:T(8,128)}, u32[]{:S(2)}, u32[]{:S(2)}) collective-permute-start(f32[1,106,1024]{2,1,0:T(8,128)} %slice.247), channel_id=1, source_target_pairs={{16,0},{32,16},{48,32},{64,48},{80,64},{96,80},{112,96},{128,112},... | collective-permute-start | bytes 1302536 | tf_op jit(solution)/shard_map/ppermute | solution.py:20
  62.0 1.9 %copy-start.7 = (f32[1,424,256]{2,1,0:T(8,128)S(1)}, f32[1,424,256]{2,1,0:T(8,128)}, u32[]{:S(2)}) copy-start(f32[1,424,256]{2,1,0:T(8,128)} %get-tuple-element.91) | copy-start | bytes 1302532
  64.1 21.9 %copy-start.9 = (bf16[360,256]{1,0:T(8,128)(2,1)S(1)}, bf16[360,256]{1,0:T(8,128)(2,1)}, u32[]{:S(2)}) copy-start(bf16[360,256]{1,0:T(8,128)(2,1)} %copy-done.8) | copy-start | bytes 552964
  64.1 21.8 %copy-start.11 = (f32[360,512]{1,0:T(8,128)S(1)}, f32[360,512]{1,0:T(8,128)}, u32[]{:S(2)}) copy-start(f32[360,512]{1,0:T(8,128)} %copy-done.10) | copy-start | bytes 2211844
  64.1 21.8 %copy-start.15 = (bf16[512,256]{1,0:T(8,128)(2,1)S(1)}, bf16[512,256]{1,0:T(8,128)(2,1)}, u32[]{:S(2)}) copy-start(bf16[512,256]{1,0:T(8,128)(2,1)} %param.26) | copy-start | bytes 786436
  81.0 8.2 %collective-permute-start.6 = (f32[4,8,1024]{2,1,0:T(8,128)}, f32[4,8,1024]{2,1,0:T(8,128)S(1)}, u32[]{:S(2)}, u32[]{:S(2)}) collective-permute-start(f32[4,8,1024]{2,1,0:T(8,128)} %get-tuple-element.93), channel_id=1, source_target_pairs={{0,1},{1,2},{2,3},{3,4},{4,5},{5,6},{6,7},{7,8},{8,9},{9,10},{10,1... | collective-permute-start | bytes 393224 | tf_op jit(solution)/shard_map/ppermute | solution.py:18
  86.3 1.0 copy-start.14
  87.3 10.8 %collective-permute-start.7 = (f32[4,8,1024]{2,1,0:T(8,128)S(1)}, f32[4,8,1024]{2,1,0:T(8,128)S(1)}, u32[]{:S(2)}, u32[]{:S(2)}) collective-permute-start(f32[4,8,1024]{2,1,0:T(8,128)S(1)} %copy-done.14), channel_id=1, source_target_pairs={{1,0},{2,1},{3,2},{4,3},{5,4},{6,5},{7,6},{8,7},{9,8},{10,9},{11,1... | collective-permute-start | bytes 393224 | tf_op jit(solution)/shard_map/ppermute | solution.py:20
  89.3 8.8 %copy-start.3 = (f32[4,90,1024]{2,1,0:T(8,128)}, f32[4,90,1024]{2,1,0:T(8,128)S(1)}, u32[]{:S(2)}) copy-start(f32[4,90,1024]{2,1,0:T(8,128)S(1)} %fusion.24) | copy-start | bytes 4423684
where the time goes:
time: 104 us; the launch traced here: 103 us
  starting transfers between devices  32.4 us (31%)
  waiting for transfers between devices  28.8 us (28%)
  local copies, waits for them, and re-layouts  26.5 us (25%)
  matrix products  8.39 us (8%)
  other arithmetic  5.62 us (5%)
  between operations  1.13 us (1%)
    ppermute x4, starting transfers between devices, padded_2(): lax.ppermute(head, axis, [((i + 1) % count, i) for i in range(ends)])  16.6 us
    ppermute x4, starting transfers between devices, padded_2(): lax.ppermute(tail, axis, [(i, (i + 1) % count) for i in range(ends)])  15.8 us
    ppermute x4, waiting for transfers between devices, padded_2(): lax.ppermute(head, axis, [((i + 1) % count, i) for i in range(ends)])  14.8 us
    ppermute x4, waiting for transfers between devices, padded_2(): lax.ppermute(tail, axis, [(i, (i + 1) % count) for i in range(ends)])  14 us
    reshape x3, local copies, waits for them, and re-layouts, spatial_sum(): source = mixed[lat_tap:lat_tap + rows].reshape(rows, span * KB, chans)  6.09 us
    slice x4, local copies, waits for them, and re-layouts, on_device(): edges = jnp.stack([partial_sums[0], partial_sums[rows + 1]])  5.59 us
    unnamed x35, local copies, waits for them, and re-layouts  3.38 us
    slice x2, local copies, waits for them, and re-layouts, on_device(): inner = partial_sums[1:rows + 1]  3.27 us
  transfers between devices with their start and end apart: 8, of which 4 were waited for; matrix products, arithmetic and copies ran while one was open for 12% of the time, Pallas kernels for 0%

commit v1 on v0

v1 whole, which is shorter than its diff:
```python
import functools

import jax
import jax.numpy as jnp
from jax import lax
from jax.experimental import pallas as pl
from jax.experimental.pallas import tpu as pltpu
from jax.sharding import PartitionSpec as P

KB = 4
REACH = 8
TAPS = 2 * REACH + 1
WIDE = 2 * REACH
CH = 256
HID = 512
ROWS = 4
RING = 128
CELLS = 112
OUTC = 96
MESH = pl.DeviceIdType.MESH
F32 = jnp.float32
BF16 = jnp.bfloat16


def dot(left, right):
    return jnp.dot(left, right, preferred_element_type=F32)


def dot_last(left, right):
    return lax.dot_general(left, right, (((1,), (1,)), ((), ())), preferred_element_type=F32)


def circulant(taps, count, start):
    spread = jnp.broadcast_to(taps, (count, RING))
    return pltpu.roll(spread, (start - REACH) % RING, 1, stride=1, stride_axis=0)


def tap_row(row, tap, basis):
    return ((2 - tap) if row in (-1, ROWS) else tap) * KB + basis


def place():
    lat, lon = lax.axis_index("lat"), lax.axis_index("lon")
    lats, lons = lax.axis_size("lat"), lax.axis_size("lon")
    odd = lax.rem(lat, 2)
    near = jnp.where(odd == 1, lat - 1, lat + 1)
    far = jnp.where(odd == 1, lat + 1, lat - 1)
    has_far = jnp.logical_and(far >= 0, far < lats)
    west = lax.rem(lon + lons - 1, lons)
    east = lax.rem(lon + 1, lons)
    return lat, lon, odd, near, far, has_far, west, east


def owned(odd, row):
    return jnp.where(odd == 1, row, ROWS - 1 - row)


def forward_kernel(
    width,
    fields_hbm, cot_hbm, w_mix_hbm, w_up_hbm, w_down_hbm, filters_ref, reach_ref,
    result_ref, grads_ref, back_ref,
    own, edge, cot_w, cot_e, taps_own, near_in, far_in, taps_near, taps_far,
    w_in, e_in, cw_in, ce_in, nw_in, ne_in, ncw_in, nce_in, fw_in, fe_in, fcw_in, fce_in,
    cells, cots, taps, taps_rev, fwd, w_mix, w_up, w_down,
    load_sem, send_sem, recv_sem,
):
    lat, lon, odd, near, far, has_far, west, east = place()

    barrier = pltpu.get_barrier_semaphore()

    def greet(target):
        pl.semaphore_signal(barrier, inc=1, device_id=target, device_id_type=MESH)

    for target in ((lat, west), (lat, east), (near, lon), (near, west), (near, east)):
        greet(target)

    @pl.when(has_far)
    def _():
        for target in ((far, lon), (far, west), (far, east)):
            greet(target)

    loads = []
    for row in range(ROWS):
        loads.append((fields_hbm.at[owned(odd, row)], own.at[1 + row]))
        loads.append((cot_hbm.at[owned(odd, row)], own.at[(0, 6, 7, 5)[row]]))
    loads += [(w_mix_hbm, w_mix), (w_up_hbm, w_up), (w_down_hbm, w_down)]
    loads = [pltpu.make_async_copy(s, d, load_sem.at[i]) for i, (s, d) in enumerate(loads)]
    for load in loads:
        load.start()

    taps[...] = jnp.zeros_like(taps)
    lane = lax.broadcasted_iota(jnp.int32, (1, TAPS), 1) - REACH
    for row in range(ROWS):
        keep = jnp.abs(lane) <= reach_ref[owned(odd, row)]
        for basis in range(KB):
            block = filters_ref[basis, owned(odd, row)].astype(F32)
            for tap in range(3):
                value = jnp.where(odd == 1, block[tap : tap + 1], block[2 - tap : 3 - tap])
                taps[1 + row, pl.ds(tap * KB + basis, 1), 0:TAPS] = jnp.where(keep, value, 0.0)
    taps_own[0] = taps[1].astype(BF16)
    taps_own[1] = taps[ROWS].astype(BF16)

    for load in loads[: 2 * ROWS]:
        load.wait()
    edge[...] = own[1:5, width - WIDE : width]
    for row, slot in enumerate((0, 6, 7, 5)):
        cot_w[row] = own[slot, 0:REACH]
        cot_e[row] = own[slot, width - REACH : width]

    pl.semaphore_wait(barrier, 5 + jnp.where(has_far, 3, 0))

    def remote(index, source, target, device):
        return pltpu.make_async_remote_copy(
            src_ref=source, dst_ref=target, send_sem=send_sem.at[index],
            recv_sem=recv_sem.at[index], device_id=device, device_id_type=MESH,
        )

    head = pl.ds(0, WIDE)
    far_sends = [
        remote(0, own.at[pl.ds(3, 3)], far_in, (far, lon)),
        remote(1, taps_own.at[1], taps_far, (far, lon)),
        remote(2, own.at[pl.ds(3, 2), head], fe_in, (far, west)),
        remote(3, cot_w.at[3], fce_in, (far, west)),
        remote(4, edge.at[pl.ds(2, 2)], fw_in, (far, east)),
        remote(5, cot_e.at[3], fcw_in, (far, east)),
    ]
    lon_sends = [
        remote(6, own.at[pl.ds(1, 4), head], e_in, (lat, west)),
        remote(7, cot_w, ce_in, (lat, west)),
        remote(8, edge, w_in, (lat, east)),
        remote(9, cot_e, cw_in, (lat, east)),
    ]
    near_sends = [
        remote(10, own.at[pl.ds(0, 3)], near_in, (near, lon)),
        remote(11, taps_own.at[0], taps_near, (near, lon)),
        remote(12, own.at[pl.ds(1, 2), head], ne_in, (near, west)),
        remote(13, cot_w.at[0], nce_in, (near, west)),
        remote(14, edge.at[pl.ds(0, 2)], nw_in, (near, east)),
        remote(15, cot_e.at[0], ncw_in, (near, east)),
    ]

    @pl.when(has_far)
    def _():
        for copy in far_sends:
            copy.start()

    for copy in lon_sends + near_sends:
        copy.start()

    @pl.when(jnp.logical_not(has_far))
    def _():
        for ref in (far_in, taps_far, fe_in, fce_in, fw_in, fcw_in):
            ref[...] = jnp.zeros_like(ref)

    first = lax.broadcasted_iota(jnp.int32, (RING, RING), 0)
    second = lax.broadcasted_iota(jnp.int32, (RING, RING), 1)
    flip = (first + second == 2 * REACH).astype(BF16)

    def reverse(row):
        taps_rev[row + 1] = dot(taps[row + 1].astype(BF16), flip)

    def forward_matrix(row):
        for tap in range(3):
            for basis in range(KB):
                line = taps[row + 1, pl.ds(tap_row(row, tap, basis), 1), :]
                block = jnp.concatenate(
                    [circulant(line, 104, 0), circulant(line, REACH, RING - REACH)], axis=0
                )
                fwd[row + 1, basis * CELLS : (basis + 1) * CELLS, tap * RING : (tap + 1) * RING] = (
                    block.astype(BF16)
                )

    def backward_blocks(source):
        for out in range(max(0, source - 1), min(ROWS, source + 2)):
            tap, slot = out - source + 1, source - out + 1
            for basis in range(KB):
                line = taps_rev[source + 1, pl.ds(tap_row(source, tap, basis), 1), :]
                back_ref[out, basis * OUTC : (basis + 1) * OUTC, slot * RING : (slot + 1) * RING] = (
                    circulant(line, OUTC, 0).astype(BF16)
                )

    for row in range(ROWS):
        reverse(row)
        forward_matrix(row)
        backward_blocks(row)

    for load in loads[2 * ROWS :]:
        load.wait()

    def fill_cells(row, middle, west_part, east_part):
        cells[row + 2, 0:width] = middle
        cells[row + 2, width : width + WIDE] = east_part
        cells[row + 2, width + WIDE : RING - WIDE] = jnp.zeros(
            (RING - 2 * WIDE - width, CH), BF16
        )
        cells[row + 2, RING - WIDE : RING] = west_part

    def fill_cots(row, middle, west_part, east_part):
        cots[row + 1, 0:width] = middle
        cots[row + 1, width : width + REACH] = east_part
        cots[row + 1, width + REACH : 104] = jnp.zeros((104 - REACH - width, CH), BF16)
        cots[row + 1, 104:CELLS] = west_part

    def advance(rows):
        count = len(rows)
        convs = []
        for row in rows:
            source = cells[row + 1 : row + 4].reshape(3 * RING, CH)
            convs.append(dot(fwd[row + 1], source).astype(BF16))
        spatial = jnp.zeros((count * CELLS, CH), F32)
        for basis in range(KB):
            part = jnp.concatenate(
                [c[basis * CELLS : (basis + 1) * CELLS] for c in convs], axis=0
            )
            spatial = spatial + dot(part, w_mix[:, basis * CH : (basis + 1) * CH])
        centre = jnp.concatenate(
            [p for row in rows for p in (cells[row + 2, 0:104].astype(F32), cells[row + 2, 120:128].astype(F32))],
            axis=0,
        )
        hidden = (centre + spatial).astype(BF16)
        pre = dot(hidden, w_up[...])
        half = 0.5 * (1.0 + lax.erf(pre * 0.7071067811865476))
        slope = half + pre * jnp.exp(-0.5 * pre * pre) * 0.3989422804014327
        upstream = jnp.concatenate([cots[row + 1] for row in rows], axis=0)
        grad_active = (dot_last(upstream, w_down[...]) * slope).astype(BF16)
        grad = (upstream.astype(F32) + dot_last(grad_active, w_up[...])).astype(BF16)
        active = (half * pre).astype(BF16)
        for n, row in enumerate(rows):
            base = n * CELLS
            grads_ref[row + 1, 0:104] = grad[base : base + 104]
            grads_ref[row + 1, 104:120] = jnp.zeros((WIDE, CH), BF16)
            grads_ref[row + 1, 120:128] = grad[base + 104 : base + CELLS]
            if 0 <= row < ROWS:
                result = hidden[base : base + OUTC].astype(F32) + dot(
                    active[base : base + OUTC], w_down[...]
                )
                result_ref[row] = result[:width].astype(BF16)

    for copy in lon_sends:
        copy.wait_recv()
    for row in range(ROWS):
        fill_cells(row, own[1 + row], w_in[row], e_in[row])
        fill_cots(row, own[(0, 6, 7, 5)[row]], cw_in[row], ce_in[row])
    advance((1, 2))

    for copy in near_sends:
        copy.wait_recv()
    taps[0] = taps_near[...].astype(F32)
    reverse(-1)
    forward_matrix(-1)
    backward_blocks(-1)
    fill_cells(-1, near_in[1], nw_in[0], ne_in[0])
    fill_cells(-2, near_in[2], nw_in[1], ne_in[1])
    fill_cots(-1, near_in[0], ncw_in[...], nce_in[...])
    advance((0, -1))

    @pl.when(has_far)
    def _():
        for copy in far_sends:
            copy.wait_recv()

    taps[ROWS + 1] = taps_far[...].astype(F32)
    reverse(ROWS)
    forward_matrix(ROWS)
    backward_blocks(ROWS)
    fill_cells(ROWS, far_in[1], fw_in[1], fe_in[1])
    fill_cells(ROWS + 1, far_in[0], fw_in[0], fe_in[0])
    fill_cots(ROWS, far_in[2], fcw_in[...], fce_in[...])
    advance((3, 4))

    for copy in lon_sends + near_sends:
        copy.wait_send()

    @pl.when(has_far)
    def _():
        for copy in far_sends:
            copy.wait_send()


def backward_kernel(width, result_in, grads_ref, back_ref, w_mix_hbm, result_hbm, grad_hbm, out, w_mix, sems):
    odd = lax.rem(lax.axis_index("lat"), 2)
    weights = pltpu.make_async_copy(w_mix_hbm, w_mix, sems.at[8])
    weights.start()
    copies = [
        pltpu.make_async_copy(result_in.at[row], result_hbm.at[owned(odd, row)], sems.at[row])
        for row in range(ROWS)
    ]
    for copy in copies:
        copy.start()
    weights.wait()
    for rows in ((0, 1), (2, 3)):
        convs = []
        for row in rows:
            source = grads_ref[row : row + 3].reshape(3 * RING, CH)
            convs.append(dot(back_ref[row], source).astype(BF16))
        total = jnp.concatenate([grads_ref[row + 1, 0:OUTC].astype(F32) for row in rows], axis=0)
        for basis in range(KB):
            part = jnp.concatenate([c[basis * OUTC : (basis + 1) * OUTC] for c in convs], axis=0)
            total = total + dot_last(part, w_mix[:, basis * CH : (basis + 1) * CH])
        for n, row in enumerate(rows):
            out[row] = total[n * OUTC : n * OUTC + width].astype(BF16)
            copy = pltpu.make_async_copy(
                out.at[row], grad_hbm.at[owned(odd, row)], sems.at[ROWS + row]
            )
            copy.start()
            copies.append(copy)
    for copy in copies:
        copy.wait()


def on_device(fields, w_mix, filters, reach, w_up, w_down, cotangent):
    rows, width, chans = fields.shape
    hbm = pl.BlockSpec(memory_space=pltpu.HBM)
    vmem = pl.BlockSpec(memory_space=pltpu.VMEM)
    smem = pl.BlockSpec(memory_space=pltpu.SMEM)

    def held(*shape, kind=BF16):
        return pltpu.VMEM(shape, kind)

    result, grads, back = pl.pallas_call(
        functools.partial(forward_kernel, width),
        name="halo_forward",
        out_shape=(
            jax.ShapeDtypeStruct((rows, width, chans), BF16),
            jax.ShapeDtypeStruct((rows + 2, RING, chans), BF16),
            jax.ShapeDtypeStruct((rows, KB * OUTC, 3 * RING), BF16),
        ),
        in_specs=[hbm] * 5 + [vmem, smem],
        out_specs=(vmem, vmem, vmem),
        scratch_shapes=[
            held(8, width, chans),
            held(rows, WIDE, chans),
            held(rows, REACH, chans),
            held(rows, REACH, chans),
            held(2, 16, RING),
            held(3, width, chans),
            held(3, width, chans),
            held(16, RING),
            held(16, RING),
            held(rows, WIDE, chans),
            held(rows, WIDE, chans),
            held(rows, REACH, chans),
            held(rows, REACH, chans),
            held(2, WIDE, chans),
            held(2, WIDE, chans),
            held(REACH, chans),
            held(REACH, chans),
            held(2, WIDE, chans),
            held(2, WIDE, chans),
            held(REACH, chans),
            held(REACH, chans),
            held(rows + 4, RING, chans),
            held(rows + 2, CELLS, chans),
            held(rows + 2, 16, RING, kind=F32),
            held(rows + 2, 16, RING, kind=F32),
            held(rows + 2, KB * CELLS, 3 * RING),
            held(chans, KB * chans),
            held(chans, HID),
            held(HID, chans),
            pltpu.SemaphoreType.DMA((11,)),
            pltpu.SemaphoreType.DMA((16,)),
            pltpu.SemaphoreType.DMA((16,)),
        ],
        compiler_params=pltpu.CompilerParams(
            collective_id=0, has_side_effects=True, vmem_limit_bytes=24 << 20
        ),
    )(fields, cotangent, w_mix, w_up, w_down, filters, reach)
    return pl.pallas_call(
        functools.partial(backward_kernel, width),
        name="transposed_mix",
        out_shape=(
            jax.ShapeDtypeStruct((rows, width, chans), BF16),
            jax.ShapeDtypeStruct((rows, width, chans), BF16),
        ),
        in_specs=[vmem, vmem, vmem, hbm],
        out_specs=(hbm, hbm),
        scratch_shapes=[
            held(rows, width, chans),
            held(chans, KB * chans),
            pltpu.SemaphoreType.DMA((9,)),
        ],
        compiler_params=pltpu.CompilerParams(vmem_limit_bytes=16 << 20),
    )(result, grads, back, w_mix)


def solution(mesh):
    return jax.shard_map(
        on_device,
        mesh=mesh,
        in_specs=(
            P("lat", "lon", None),
            P(),
            P(None, "lat", None, None),
            P("lat"),
            P(),
            P(),
            P("lat", "lon", None),
        ),
        out_specs=(P("lat", "lon", None), P("lat", "lon", None)),
        check_vma=False,
    )
```

time: 104 us -> 36.9 us (0.35)
  the two profiles are of different devices: /device:TPU:318 before, /device:TPU:1 now
where the time goes in v1:
time: 36.9 us; the launch traced here: 36.6 us
  Pallas kernels  28.1 us (76%)
  local copies, waits for them, and re-layouts  7.83 us (21%)
  between operations  0.66 us (2%)
    pallas_call x1, Pallas kernels, on_device(): pl.pallas_call(functools.partial(forward_kernel, width), name='halo_forwa...  26 us
    unnamed x11, local copies, waits for them, and re-layouts  6.2 us
    pallas_call x1, Pallas kernels, on_device(): pl.pallas_call(functools.partial(backward_kernel, width), name='transpose...  2.05 us
    pallas_call x2, local copies, waits for them, and re-layouts, on_device(): pl.pallas_call(functools.partial(backward_kernel, width), name='transpose...  1.63 us

profile of v1, /device:TPU:1, one launch (start us, length us, event | category | flops | bytes accessed | tf_op | source)
XLA Modules:
  0.0 36.6 jit_solution(1234572974827022702)
XLA Ops:
  0.6 0.7 %copy.11.filters_ref = bf16[4,4,3,17]{3,2,1,0:T(4,128)(2,1)S(1)} copy(bf16[4,4,3,17]{3,1,2,0:T(4,128)(2,1)} %param.9) | data formatting | bytes 3264 | tf_op args[2]
  1.3 0.9 %copy.9.fields_hbm = bf16[4,90,256]{2,1,0:T(8,128)(2,1)S(1)} copy(bf16[4,90,256]{2,0,1:T(4,128)(2,1)} %param.7) | data formatting | bytes 368640 | tf_op args[0]
  2.3 0.9 %copy.10.cot_hbm = bf16[4,90,256]{2,1,0:T(8,128)(2,1)S(1)} copy(bf16[4,90,256]{2,0,1:T(4,128)(2,1)} %param.13) | data formatting | bytes 368640 | tf_op args[6]
  3.2 0.0 copy-start
  3.3 1.0 %copy-done = bf16[256,1024]{1,0:T(8,128)(2,1)S(1)} copy-done((bf16[256,1024]{1,0:T(8,128)(2,1)S(1)}, bf16[256,1024]{1,0:T(8,128)(2,1)}, u32[]{:S(2)}) %copy-start) | copy-done | bytes 524312
  4.3 0.0 copy-start.1
  4.3 0.9 %copy-done.1 = bf16[256,512]{1,0:T(8,128)(2,1)S(1)} copy-done((bf16[256,512]{1,0:T(8,128)(2,1)S(1)}, bf16[256,512]{1,0:T(8,128)(2,1)}, u32[]{:S(2)}) %copy-start.1) | copy-done | bytes 262168
  5.2 0.0 copy-start.2
  5.2 0.9 %copy-done.2 = bf16[512,256]{1,0:T(8,128)(2,1)S(1)} copy-done((bf16[512,256]{1,0:T(8,128)(2,1)S(1)}, bf16[512,256]{1,0:T(8,128)(2,1)}, u32[]{:S(2)}) %copy-start.2) | copy-done | bytes 262168
  6.2 0.0 copy-start.3
  6.2 0.7 %copy-done.3 = s32[4]{0:T(128)S(1)} copy-done((s32[4]{0:T(128)S(1)}, s32[4]{0:T(128)}, u32[]{:S(2)}) %copy-start.3) | copy-done | bytes 40
  6.8 26.0 %halo_forward.1 = (bf16[4,90,256]{2,1,0:T(8,128)(2,1)S(1)}, bf16[6,128,256]{2,1,0:T(8,128)(2,1)S(1)}, bf16[4,384,384]{2,1,0:T(8,128)(2,1)S(1)}) custom-call(bf16[4,90,256]{2,1,0:T(8,128)(2,1)S(1)} %copy.9.fields_hbm, bf16[4,90,256]{2,1,0:T(8,128)(2,1)S(1)} %copy.10.cot_hbm, bf16[256,1024]{1,0:T(8,128)(2,1)S(1)} %copy-done, bf16[256,512]{1,0:T(8,128)(2,1)S(1)} %copy-done.1, ...), custom_call_target="tpu_custom_call" | custom-call | tf_op jit(solution)/shard_map/halo_forward/pallas_call | solution.py:320
  32.9 2.0 %transposed_mix.1 = (bf16[4,90,256]{2,1,0:T(8,128)(2,1)S(1)}, bf16[4,90,256]{2,1,0:T(8,128)(2,1)S(1)}) custom-call(bf16[4,90,256]{2,1,0:T(8,128)(2,1)S(1)} %get-tuple-element.5.result_in, bf16[6,128,256]{2,1,0:T(8,128)(2,1)S(1)} %get-tuple-element.6.grads_ref, bf16[4,384,384]{2,1,0:T(8,128)(2,1)S(1)} %get-tuple-element.7.back_ref, bf16[256,1024]{1,0:T(8,128)(2,1)S(1)} %copy-done), custom_call_target="tpu_custom_call" | custom-call | tf_op jit(solution)/shard_map/transposed_mix/pallas_call | solution.py:368
  35.0 0.8 %copy.12 = bf16[4,90,256]{2,0,1:T(4,128)(2,1)} copy(bf16[4,90,256]{2,1,0:T(8,128)(2,1)S(1)} %get-tuple-element.8) | data formatting | bytes 368640 | tf_op jit(solution)/shard_map/transposed_mix/pallas_call | solution.py:368
  35.8 0.8 %copy.13 = bf16[4,90,256]{2,0,1:T(4,128)(2,1)} copy(bf16[4,90,256]{2,1,0:T(8,128)(2,1)S(1)} %get-tuple-element.9) | data formatting | bytes 368640 | tf_op jit(solution)/shard_map/transposed_mix/pallas_call | solution.py:368
Async XLA Ops:
  3.2 1.0 %copy-start = (bf16[256,1024]{1,0:T(8,128)(2,1)S(1)}, bf16[256,1024]{1,0:T(8,128)(2,1)}, u32[]{:S(2)}) copy-start(bf16[256,1024]{1,0:T(8,128)(2,1)} %w_mix_hbm.3) | copy-start | bytes 1572868
  4.3 0.9 %copy-start.1 = (bf16[256,512]{1,0:T(8,128)(2,1)S(1)}, bf16[256,512]{1,0:T(8,128)(2,1)}, u32[]{:S(2)}) copy-start(bf16[256,512]{1,0:T(8,128)(2,1)} %w_up_hbm.1) | copy-start | bytes 786436
  5.2 0.9 %copy-start.2 = (bf16[512,256]{1,0:T(8,128)(2,1)S(1)}, bf16[512,256]{1,0:T(8,128)(2,1)}, u32[]{:S(2)}) copy-start(bf16[512,256]{1,0:T(8,128)(2,1)} %w_down_hbm.1) | copy-start | bytes 786436
  6.2 0.7 %copy-start.3 = (s32[4]{0:T(128)S(1)}, s32[4]{0:T(128)}, u32[]{:S(2)}) copy-start(s32[4]{0:T(128)} %reach_ref.1) | copy-start | bytes 52

commit v2 on v1

v2 whole, which is shorter than its diff:
```python
import functools

import jax
import jax.numpy as jnp
from jax import lax
from jax.experimental import pallas as pl
from jax.experimental.pallas import tpu as pltpu
from jax.sharding import PartitionSpec as P

KB = 4
REACH = 8
TAPS = 2 * REACH + 1
WIDE = 2 * REACH
CH = 256
HID = 512
ROWS = 4
LANES = 128
RING = 128
CELLS = 112
OUTC = 96
MESH = pl.DeviceIdType.MESH
F32 = jnp.float32
BF16 = jnp.bfloat16


def dot(left, right):
    return jnp.dot(left, right, preferred_element_type=F32)


def dot_last(left, right):
    return lax.dot_general(left, right, (((1,), (1,)), ((), ())), preferred_element_type=F32)


def circulant(taps, count, start):
    spread = jnp.broadcast_to(taps, (count, RING))
    return pltpu.roll(spread, (start - REACH) % RING, 1, stride=1, stride_axis=0)


def packed(grid):
    rows, width, chans = grid.shape
    tiles = grid.transpose(1, 0, 2).reshape(width, rows, chans // LANES, LANES)
    return tiles.transpose(0, 2, 1, 3).reshape(width * rows * chans // LANES, LANES)


def unpacked(tiles, rows, width, chans):
    grid = tiles.reshape(width, chans // LANES, rows, LANES).transpose(0, 2, 1, 3)
    return grid.reshape(width, rows, chans).transpose(1, 0, 2)


def read_row(tiles, row, width):
    return jnp.concatenate(
        [tiles[pl.ds(half * ROWS + row, width, stride=2 * ROWS), :] for half in range(2)], axis=1
    )


def write_row(tiles, row, width, value):
    for half in range(2):
        tiles[pl.ds(half * ROWS + row, width, stride=2 * ROWS), :] = value[
            :, half * LANES : (half + 1) * LANES
        ]


def place():
    lat, lon = lax.axis_index("lat"), lax.axis_index("lon")
    lats, lons = lax.axis_size("lat"), lax.axis_size("lon")
    odd = lax.rem(lat, 2)
    near = jnp.where(odd == 1, lat - 1, lat + 1)
    far = jnp.where(odd == 1, lat + 1, lat - 1)
    has_far = jnp.logical_and(far >= 0, far < lats)
    west = lax.rem(lon + lons - 1, lons)
    east = lax.rem(lon + 1, lons)
    return lat, lon, odd, near, far, has_far, west, east


def owned(odd, row):
    return jnp.where(odd == 1, row, ROWS - 1 - row)


def forward_kernel(
    width,
    fields_hbm, cot_hbm, w_mix_hbm, w_up_hbm, w_down_hbm, filters_hbm, reach_hbm,
    result_ref, grads_ref, back_ref, w_mix, done_ref,
    raw, raw_cot, wide, filters_ref, filters_wide, reach_ref,
    own, edge, cot_w, cot_e, taps_own, near_in, far_in, taps_near, taps_far,
    w_in, e_in, cw_in, ce_in, nw_in, ne_in, ncw_in, nce_in, fw_in, fe_in, fcw_in, fce_in,
    cells, cots, taps, taps_rev, fwd, partial_ref, w_up, w_down,
    load_sem, send_sem, recv_sem,
):
    lat, lon, odd, near, far, has_far, west, east = place()

    barrier = pltpu.get_barrier_semaphore()

    def greet(target):
        pl.semaphore_signal(barrier, inc=1, device_id=target, device_id_type=MESH)

    last = jnp.logical_and(lat == 0, lon == 0)
    close = ((lat, west), (lat, east), (near, lon), (near, west), (near, east))
    to_last = [jnp.logical_and(a == 0, o == 0) for a, o in close]
    n_last = sum(flag.astype(jnp.int32) for flag in to_last)
    for target, flag in zip(close, to_last):
        pl.when(jnp.logical_not(jnp.logical_or(last, flag)))(functools.partial(greet, target))

    @pl.when(has_far)
    def _():
        for target in ((far, lon), (far, west), (far, east)):
            greet(target)

    loads = [
        (fields_hbm, raw), (cot_hbm, raw_cot), (filters_hbm, filters_ref), (reach_hbm, reach_ref),
        (w_mix_hbm, w_mix), (w_up_hbm, w_up), (w_down_hbm, w_down),
    ]
    loads = [pltpu.make_async_copy(s, d, load_sem.at[i]) for i, (s, d) in enumerate(loads)]
    for load in loads:
        load.start()

    for load, source, slots in ((loads[0], raw, (1, 2, 3, 4)), (loads[1], raw_cot, (0, 6, 7, 5))):
        load.wait()
        wide[...] = source[...].astype(F32)
        for row in range(ROWS):
            own[slots[row]] = read_row(wide, owned(odd, row), width).astype(BF16)

    loads[2].wait()
    loads[3].wait()
    taps[...] = jnp.zeros_like(taps)
    filters_wide[...] = filters_ref[...].astype(F32)
    lane = lax.broadcasted_iota(jnp.int32, (1, TAPS), 1) - REACH
    for row in range(ROWS):
        keep = jnp.abs(lane) <= reach_ref[owned(odd, row)]
        lines = filters_wide[pl.ds(owned(odd, row), 3 * KB, stride=ROWS), :]
        taps[1 + row, 0 : 3 * KB, 0:TAPS] = jnp.where(keep, lines, 0.0)
    taps_own[0] = taps[1].astype(BF16)
    taps_own[1] = taps[ROWS].astype(BF16)

    edge[...] = own[1:5, width - WIDE : width]
    for row, slot in enumerate((0, 6, 7, 5)):
        cot_w[row] = own[slot, 0:REACH]
        cot_e[row] = own[slot, width - REACH : width]

    pl.semaphore_wait(barrier, 5 - n_last + jnp.where(has_far, 3, 0))
    for target, flag in zip(close, to_last):
        pl.when(jnp.logical_or(last, flag))(functools.partial(greet, target))

    def remote(index, source, target, device):
        return pltpu.make_async_remote_copy(
            src_ref=source, dst_ref=target, send_sem=send_sem.at[index],
            recv_sem=recv_sem.at[index], device_id=device, device_id_type=MESH,
        )

    head = pl.ds(0, WIDE)
    far_sends = [
        remote(0, taps_own.at[1], taps_far, (far, lon)),
        remote(1, own.at[pl.ds(3, 3)], far_in, (far, lon)),
        remote(2, own.at[pl.ds(3, 2), head], fe_in, (far, west)),
        remote(3, cot_w.at[3], fce_in, (far, west)),
        remote(4, edge.at[pl.ds(2, 2)], fw_in, (far, east)),
        remote(5, cot_e.at[3], fcw_in, (far, east)),
    ]
    west_sends = [
        remote(6, own.at[pl.ds(1, 4), head], e_in, close[0]),
        remote(7, cot_w, ce_in, close[0]),
    ]
    east_sends = [
        remote(8, edge, w_in, close[1]),
        remote(9, cot_e, cw_in, close[1]),
    ]
    mate_sends = [
        remote(10, taps_own.at[0], taps_near, close[2]),
        remote(11, own.at[pl.ds(0, 3)], near_in, close[2]),
    ]
    mate_west_sends = [
        remote(12, own.at[pl.ds(1, 2), head], ne_in, close[3]),
        remote(13, cot_w.at[0], nce_in, close[3]),
    ]
    mate_east_sends = [
        remote(14, edge.at[pl.ds(0, 2)], nw_in, close[4]),
        remote(15, cot_e.at[0], ncw_in, close[4]),
    ]
    groups = (west_sends, east_sends, mate_sends, mate_west_sends, mate_east_sends)
    lon_sends = west_sends + east_sends
    near_sends = mate_sends + mate_west_sends + mate_east_sends

    def start(copies):
        for copy in copies:
            copy.start()

    pl.when(has_far)(functools.partial(start, far_sends[:1] + far_sends[2:]))
    for copies, flag in zip(groups, to_last):
        pl.when(jnp.logical_not(flag))(functools.partial(start, copies))
    pl.when(has_far)(functools.partial(start, far_sends[1:2]))

    @pl.when(n_last > 0)
    def _():
        pl.semaphore_wait(barrier, n_last)

    for copies, flag in zip(groups, to_last):
        pl.when(flag)(functools.partial(start, copies))

    @pl.when(jnp.logical_not(has_far))
    def _():
        for ref in (far_in, taps_far, fe_in, fce_in, fw_in, fcw_in):
            ref[...] = jnp.zeros_like(ref)

    first = lax.broadcasted_iota(jnp.int32, (RING, RING), 0)
    second = lax.broadcasted_iota(jnp.int32, (RING, RING), 1)
    flip = (first + second == 2 * REACH).astype(BF16)

    def tap_line(tap, basis):
        return basis * 3 + jnp.where(odd == 1, tap, 2 - tap)

    def reverse(row):
        taps_rev[row + 1] = dot(taps[row + 1].astype(BF16), flip)

    def forward_matrix(row):
        for tap in range(3):
            for basis in range(KB):
                line = taps[row + 1, pl.ds(tap_line(tap, basis), 1), :]
                block = jnp.concatenate(
                    [circulant(line, 104, 0), circulant(line, REACH, RING - REACH)], axis=0
                )
                fwd[row + 1, basis * CELLS : (basis + 1) * CELLS, tap * RING : (tap + 1) * RING] = (
                    block.astype(BF16)
                )

    def backward_blocks(source):
        for out in range(max(0, source - 1), min(ROWS, source + 2)):
            tap, slot = out - source + 1, source - out + 1
            for basis in range(KB):
                line = taps_rev[source + 1, pl.ds(tap_line(tap, basis), 1), :]
                back_ref[out, basis * OUTC : (basis + 1) * OUTC, slot * RING : (slot + 1) * RING] = (
                    circulant(line, OUTC, 0).astype(BF16)
                )

    for row in range(ROWS):
        reverse(row)
        forward_matrix(row)
        backward_blocks(row)

    for load in loads[4:]:
        load.wait()

    def fill_cells(row, middle, west_part, east_part):
        cells[row + 2, 0:width] = middle
        cells[row + 2, width : width + WIDE] = east_part
        cells[row + 2, width + WIDE : RING - WIDE] = jnp.zeros(
            (RING - 2 * WIDE - width, CH), BF16
        )
        cells[row + 2, RING - WIDE : RING] = west_part

    def fill_cots(row, middle, west_part, east_part):
        cots[row + 1, 0:width] = middle
        cots[row + 1, width : width + REACH] = east_part
        cots[row + 1, width + REACH : 104] = jnp.zeros((104 - REACH - width, CH), BF16)
        cots[row + 1, 104:CELLS] = west_part

    def conv_part(row, begin, end):
        source = cells[row + 1 + begin : row + 1 + end].reshape((end - begin) * RING, CH)
        return dot(fwd[row + 1, :, begin * RING : end * RING], source)

    def advance(rows, ready=None):
        count = len(rows)
        convs = []
        for n, row in enumerate(rows):
            if ready is None:
                conv = conv_part(row, 0, 3)
            else:
                conv = partial_ref[n] + conv_part(row, ready[n], 3)
            convs.append(conv.astype(BF16))
        spatial = jnp.zeros((count * CELLS, CH), F32)
        for basis in range(KB):
            part = jnp.concatenate(
                [c[basis * CELLS : (basis + 1) * CELLS] for c in convs], axis=0
            )
            spatial = spatial + dot(part, w_mix[:, basis * CH : (basis + 1) * CH])
        centre = jnp.concatenate(
            [p for row in rows for p in (cells[row + 2, 0:104].astype(F32), cells[row + 2, 120:128].astype(F32))],
            axis=0,
        )
        hidden = (centre + spatial).astype(BF16)
        pre = dot(hidden, w_up[...])
        half = 0.5 * (1.0 + lax.erf(pre * 0.7071067811865476))
        slope = half + pre * jnp.exp(-0.5 * pre * pre) * 0.3989422804014327
        upstream = jnp.concatenate([cots[row + 1] for row in rows], axis=0)
        grad_active = (dot_last(upstream, w_down[...]) * slope).astype(BF16)
        grad = (upstream.astype(F32) + dot_last(grad_active, w_up[...])).astype(BF16)
        active = (half * pre).astype(BF16)
        for n, row in enumerate(rows):
            base = n * CELLS
            grads_ref[row + 1, 0:104] = grad[base : base + 104]
            grads_ref[row + 1, 104:120] = jnp.zeros((WIDE, CH), BF16)
            grads_ref[row + 1, 120:128] = grad[base + 104 : base + CELLS]
            if 0 <= row < ROWS:
                result = hidden[base : base + OUTC].astype(F32) + dot(
                    active[base : base + OUTC], w_down[...]
                )
                write_row(wide, owned(odd, row), width, result[:width])

    def finish(rows):
        return retreat(rows, grads_ref, back_ref, w_mix)

    for copy in lon_sends:
        copy.wait_recv()
    for row in range(ROWS):
        fill_cells(row, own[1 + row], w_in[row], e_in[row])
        fill_cots(row, own[(0, 6, 7, 5)[row]], cw_in[row], ce_in[row])
    advance((1, 2))

    mate_sends[0].wait_recv()
    taps[0] = taps_near[...].astype(F32)
    reverse(-1)
    forward_matrix(-1)
    backward_blocks(-1)
    for copy in near_sends[1:]:
        copy.wait_recv()
    fill_cells(-1, near_in[1], nw_in[0], ne_in[0])
    fill_cells(-2, near_in[2], nw_in[1], ne_in[1])
    fill_cots(-1, near_in[0], ncw_in[...], nce_in[...])
    advance((0, -1))
    done_ref[...] = finish((0, 1))

    pl.when(has_far)(far_sends[0].wait_recv)
    taps[ROWS + 1] = taps_far[...].astype(F32)
    reverse(ROWS)
    forward_matrix(ROWS)
    backward_blocks(ROWS)
    partial_ref[0] = conv_part(ROWS - 1, 0, 2)
    partial_ref[1] = conv_part(ROWS, 0, 1)

    @pl.when(has_far)
    def _():
        for copy in far_sends[1:]:
            copy.wait_recv()

    fill_cells(ROWS, far_in[1], fw_in[1], fe_in[1])
    fill_cells(ROWS + 1, far_in[0], fw_in[0], fe_in[0])
    fill_cots(ROWS, far_in[2], fcw_in[...], fce_in[...])
    advance((ROWS - 1, ROWS), ready=(2, 1))
    result_ref[...] = wide[...].astype(BF16)

    for copies in groups:
        for copy in copies:
            copy.wait_send()

    @pl.when(has_far)
    def _():
        for copy in far_sends:
            copy.wait_send()


def retreat(rows, grads_ref, back_ref, w_mix):
    convs = []
    for row in rows:
        source = grads_ref[row : row + 3].reshape(3 * RING, CH)
        convs.append(dot(back_ref[row], source).astype(BF16))
    total = jnp.concatenate([grads_ref[row + 1, 0:OUTC].astype(F32) for row in rows], axis=0)
    for basis in range(KB):
        part = jnp.concatenate([c[basis * OUTC : (basis + 1) * OUTC] for c in convs], axis=0)
        total = total + dot_last(part, w_mix[:, basis * CH : (basis + 1) * CH])
    return total


def backward_kernel(
    width, packed_result, grads_ref, back_ref, w_mix, done_ref, result_hbm, grad_hbm, wide, out, sems
):
    odd = lax.rem(lax.axis_index("lat"), 2)
    store_result = pltpu.make_async_copy(packed_result, result_hbm, sems.at[0])
    store_result.start()
    total = retreat((2, 3), grads_ref, back_ref, w_mix)
    for row in (0, 1):
        write_row(wide, owned(odd, row), width, done_ref[row * OUTC : row * OUTC + width])
        write_row(wide, owned(odd, 2 + row), width, total[row * OUTC : row * OUTC + width])
    out[...] = wide[...].astype(BF16)
    store_grad = pltpu.make_async_copy(out, grad_hbm, sems.at[1])
    store_grad.start()
    store_result.wait()
    store_grad.wait()


def on_device(fields, w_mix, filters, reach, w_up, w_down, cotangent):
    rows, width, chans = fields.shape
    hbm = pl.BlockSpec(memory_space=pltpu.HBM)
    vmem = pl.BlockSpec(memory_space=pltpu.VMEM)
    tiles = (width * rows * chans // LANES, LANES)

    def held(*shape, kind=BF16):
        return pltpu.VMEM(shape, kind)

    sources = (
        packed(fields), packed(cotangent), w_mix, w_up, w_down,
        filters.transpose(0, 2, 1, 3).reshape(3 * KB * rows, TAPS), reach,
    )
    sources = [pltpu.with_memory_space_constraint(source, pltpu.HBM) for source in sources]
    result, grads, back, held_mix, done = pl.pallas_call(
        functools.partial(forward_kernel, width),
        name="halo_forward",
        out_shape=(
            held(*tiles),
            held(rows + 2, RING, chans),
            held(rows, KB * OUTC, 3 * RING),
            held(chans, KB * chans),
            held(2 * OUTC, chans, kind=F32),
        ),
        in_specs=[hbm] * 7,
        out_specs=(vmem,) * 5,
        scratch_shapes=[
            held(*tiles),
            held(*tiles),
            held(*tiles, kind=F32),
            held(3 * KB * rows, TAPS),
            held(3 * KB * rows, TAPS, kind=F32),
            pltpu.SMEM((rows,), jnp.int32),
            held(8, width, chans),
            held(rows, WIDE, chans),
            held(rows, REACH, chans),
            held(rows, REACH, chans),
            held(2, 16, RING),
            held(3, width, chans),
            held(3, width, chans),
            held(16, RING),
            held(16, RING),
            held(rows, WIDE, chans),
            held(rows, WIDE, chans),
            held(rows, REACH, chans),
            held(rows, REACH, chans),
            held(2, WIDE, chans),
            held(2, WIDE, chans),
            held(REACH, chans),
            held(REACH, chans),
            held(2, WIDE, chans),
            held(2, WIDE, chans),
            held(REACH, chans),
            held(REACH, chans),
            held(rows + 4, RING, chans),
            held(rows + 2, CELLS, chans),
            held(rows + 2, 16, RING, kind=F32),
            held(rows + 2, 16, RING, kind=F32),
            held(rows + 2, KB * CELLS, 3 * RING),
            held(2, KB * CELLS, chans, kind=F32),
            held(chans, HID),
            held(HID, chans),
            pltpu.SemaphoreType.DMA((7,)),
            pltpu.SemaphoreType.DMA((16,)),
            pltpu.SemaphoreType.DMA((16,)),
        ],
        compiler_params=pltpu.CompilerParams(
            collective_id=0, has_side_effects=True, vmem_limit_bytes=24 << 20
        ),
    )(*sources)
    result, field_grad = pl.pallas_call(
        functools.partial(backward_kernel, width),
        name="transposed_mix",
        out_shape=(pltpu.HBM(tiles, BF16), pltpu.HBM(tiles, BF16)),
        in_specs=[vmem] * 5,
        out_specs=(hbm, hbm),
        scratch_shapes=[
            held(*tiles, kind=F32),
            held(*tiles),
            pltpu.SemaphoreType.DMA((2,)),
        ],
        compiler_params=pltpu.CompilerParams(vmem_limit_bytes=16 << 20),
    )(result, grads, back, held_mix, done)
    return unpacked(result, rows, width, chans), unpacked(field_grad, rows, width, chans)


def solution(mesh):
    return jax.shard_map(
        on_device,
        mesh=mesh,
        in_specs=(
            P("lat", "lon", None),
            P(),
            P(None, "lat", None, None),
            P("lat"),
            P(),
            P(),
            P("lat", "lon", None),
        ),
        out_specs=(P("lat", "lon", None), P("lat", "lon", None)),
        check_vma=False,
    )
```

time: 36.9 us -> 26.2 us (0.71)
  the two profiles are of different devices: /device:TPU:1 before, /device:TPU:513 now
where the time goes in v2:
time: 26.2 us; the launch traced here: 26 us
  Pallas kernels  25.4 us (97%)
  between operations  0.64 us (2%)
    pallas_call x1, Pallas kernels, on_device(): pl.pallas_call(functools.partial(forward_kernel, width), name='halo_forwa...  24 us
    pallas_call x1, Pallas kernels, on_device(): pl.pallas_call(functools.partial(backward_kernel, width), name='transpose...  1.42 us

profile of v2, /device:TPU:513, one launch (start us, length us, event | category | flops | bytes accessed | tf_op | source)
XLA Modules:
  0.0 26.0 jit_solution(5138408194261032152)
XLA Ops:
  0.6 24.0 %halo_forward.1 = (bf16[720,128]{1,0:T(8,128)(2,1)S(1)}, bf16[6,128,256]{2,1,0:T(8,128)(2,1)S(1)}, bf16[4,384,384]{2,1,0:T(8,128)(2,1)S(1)}, bf16[256,1024]{1,0:T(8,128)(2,1)S(1)}, f32[192,256]{1,0:T(8,128)S(1)}) custom-call(bf16[720,128]{1,0:T(8,128)(2,1)} %bitcast.31, bf16[720,128]{1,0:T(8,128)(2,1)} %bitcast.32, bf16[256,1024]{1,0:T(8,128)(2,1)} %w_mix_hbm.1, ...), custom_call_target="tpu_custom_call" | custom-call | tf_op jit(solution)/shard_map/halo_forward/pallas_call | solution.py:392
  24.6 1.4 %transposed_mix.1 = (bf16[720,128]{1,0:T(8,128)(2,1)}, bf16[720,128]{1,0:T(8,128)(2,1)}) custom-call(bf16[720,128]{1,0:T(8,128)(2,1)S(1)} %get-tuple-element.9.packed_result, bf16[6,128,256]{2,1,0:T(8,128)(2,1)S(1)} %get-tuple-element.10.grads_ref, bf16[4,384,384]{2,1,0:T(8,128)(2,1)S(1)} %get-tuple-element.11.back_ref, ...), custom_call_target="tpu_custom_call" | custom-call | tf_op jit(solution)/shard_map/transposed_mix/pallas_call | solution.py:448

commit v3 on v2

--- a/solution.py
+++ b/solution.py
@@ -84,26 +84,54 @@
     own, edge, cot_w, cot_e, taps_own, near_in, far_in, taps_near, taps_far,
     w_in, e_in, cw_in, ce_in, nw_in, ne_in, ncw_in, nce_in, fw_in, fe_in, fcw_in, fce_in,
     cells, cots, taps, taps_rev, fwd, partial_ref, w_up, w_down,
-    load_sem, send_sem, recv_sem,
+    load_sem, send_sem, recv_sem, told,
 ):
     lat, lon, odd, near, far, has_far, west, east = place()
 
     barrier = pltpu.get_barrier_semaphore()
+    lons = lax.axis_size("lon")
+    even = odd == 0
+    upper = lax.rem(lat, 4) >= 2
+    even_lat = lat - odd
+    desk = even_lat + 1
+    far_even = far - lax.rem(far, 2)
+    origin = jnp.logical_and(lat == 0, lon == 0)
+    origin_mate = jnp.logical_and(lat == 1, lon == 0)
+    beside = jnp.logical_or(lon == 1, lon == lons - 1)
+    beside_desk = jnp.logical_and(lat == 1, beside)
+    beside_even = jnp.logical_and(lat == 0, beside)
+    mate = (near, lon)
+    root = (0, 0)
+
+    def both(left, right):
+        return jnp.logical_and(left, right)
+
+    def no(flag):
+        return jnp.logical_not(flag)
 
     def greet(target):
         pl.semaphore_signal(barrier, inc=1, device_id=target, device_id_type=MESH)
 
-    last = jnp.logical_and(lat == 0, lon == 0)
-    close = ((lat, west), (lat, east), (near, lon), (near, west), (near, east))
-    to_last = [jnp.logical_and(a == 0, o == 0) for a, o in close]
-    n_last = sum(flag.astype(jnp.int32) for flag in to_last)
-    for target, flag in zip(close, to_last):
-        pl.when(jnp.logical_not(jnp.logical_or(last, flag)))(functools.partial(greet, target))
+    def tell(index):
+        pl.semaphore_signal(told.at[index], inc=1, device_id=mate, device_id_type=MESH)
+
+    @pl.when(both(no(origin), no(origin_mate)))
+    def _():
+        greet(mate)
+
+    @pl.when(no(origin))
+    def _():
+        greet((desk, west))
+        greet((desk, east))
 
     @pl.when(has_far)
     def _():
-        for target in ((far, lon), (far, west), (far, east)):
+        for target in ((far_even, lon), (far_even, west), (far_even, east)):
             greet(target)
+
+    fars = jnp.where(even_lat > 0, 1, 0) + jnp.where(desk < lax.axis_size("lat") - 1, 1, 0)
+    even_count = 1 + 3 * fars + jnp.where(origin, 2, 0)
+    odd_count = 5 - jnp.where(jnp.logical_or(origin_mate, beside_desk), 1, 0)
 
     loads = [
         (fields_hbm, raw), (cot_hbm, raw_cot), (filters_hbm, filters_ref), (reach_hbm, reach_ref),
@@ -136,64 +164,95 @@
         cot_w[row] = own[slot, 0:REACH]
         cot_e[row] = own[slot, width - REACH : width]
 
-    pl.semaphore_wait(barrier, 5 - n_last + jnp.where(has_far, 3, 0))
-    for target, flag in zip(close, to_last):
-        pl.when(jnp.logical_or(last, flag))(functools.partial(greet, target))
-
-    def remote(index, source, target, device):
+    def remote(index, source, target, device, arrive=None):
         return pltpu.make_async_remote_copy(
             src_ref=source, dst_ref=target, send_sem=send_sem.at[index],
-            recv_sem=recv_sem.at[index], device_id=device, device_id_type=MESH,
+            recv_sem=recv_sem.at[index if arrive is None else arrive], device_id=device, device_id_type=MESH,
         )
 
     head = pl.ds(0, WIDE)
     far_sends = [
         remote(0, taps_own.at[1], taps_far, (far, lon)),
-        remote(1, own.at[pl.ds(3, 3)], far_in, (far, lon)),
+        remote(1, own.at[pl.ds(3, 2)], far_in.at[pl.ds(0, 2)], (far, lon)),
         remote(2, own.at[pl.ds(3, 2), head], fe_in, (far, west)),
         remote(3, cot_w.at[3], fce_in, (far, west)),
         remote(4, edge.at[pl.ds(2, 2)], fw_in, (far, east)),
         remote(5, cot_e.at[3], fcw_in, (far, east)),
+        remote(16, own.at[5], far_in.at[2], (far, lon)),
     ]
     west_sends = [
-        remote(6, own.at[pl.ds(1, 4), head], e_in, close[0]),
-        remote(7, cot_w, ce_in, close[0]),
+        remote(6, own.at[pl.ds(1, 4), head], e_in, (lat, west)),
+        remote(7, cot_w, ce_in, (lat, west)),
     ]
     east_sends = [
-        remote(8, edge, w_in, close[1]),
-        remote(9, cot_e, cw_in, close[1]),
+        remote(8, edge, w_in, (lat, east)),
+        remote(9, cot_e, cw_in, (lat, east)),
     ]
     mate_sends = [
-        remote(10, taps_own.at[0], taps_near, close[2]),
-        remote(11, own.at[pl.ds(0, 3)], near_in, close[2]),
-    ]
-    mate_west_sends = [
-        remote(12, own.at[pl.ds(1, 2), head], ne_in, close[3]),
-        remote(13, cot_w.at[0], nce_in, close[3]),
-    ]
-    mate_east_sends = [
-        remote(14, edge.at[pl.ds(0, 2)], nw_in, close[4]),
-        remote(15, cot_e.at[0], ncw_in, close[4]),
-    ]
-    groups = (west_sends, east_sends, mate_sends, mate_west_sends, mate_east_sends)
+        remote(10, taps_own.at[0], taps_near, mate),
+        remote(11, own.at[pl.ds(0, 3)], near_in, mate),
+    ]
+    corner_sends = [
+        remote(12, e_in.at[pl.ds(0, 2)], ne_in, mate),
+        remote(13, ce_in.at[0], nce_in, mate),
+        remote(14, w_in.at[pl.ds(0, 2)], nw_in, mate),
+        remote(15, cw_in.at[0], ncw_in, mate),
+    ]
+    corner_west_sends = [
+        remote(17, own.at[pl.ds(1, 2), head], ne_in, (near, west), 12),
+        remote(18, cot_w.at[0], nce_in, (near, west), 13),
+    ]
+    corner_east_sends = [
+        remote(19, edge.at[pl.ds(0, 2)], nw_in, (near, east), 14),
+        remote(20, cot_e.at[0], ncw_in, (near, east), 15),
+    ]
+    corner_west = both(beside_even, lon == 1)
+    corner_east = both(beside_even, lon == lons - 1)
+    groups = (west_sends, east_sends, mate_sends)
     lon_sends = west_sends + east_sends
-    near_sends = mate_sends + mate_west_sends + mate_east_sends
+    near_sends = mate_sends + corner_sends
 
     def start(copies):
         for copy in copies:
             copy.start()
 
-    pl.when(has_far)(functools.partial(start, far_sends[:1] + far_sends[2:]))
-    for copies, flag in zip(groups, to_last):
-        pl.when(jnp.logical_not(flag))(functools.partial(start, copies))
-    pl.when(has_far)(functools.partial(start, far_sends[1:2]))
-
-    @pl.when(n_last > 0)
-    def _():
-        pl.semaphore_wait(barrier, n_last)
-
-    for copies, flag in zip(groups, to_last):
-        pl.when(flag)(functools.partial(start, copies))
+    def start_sides():
+        west_last, east_last = lon == 1, lon == lons - 1
+        pl.when(no(both(beside_even, west_last)))(functools.partial(start, west_sends))
+        pl.when(no(both(beside_even, east_last)))(functools.partial(start, east_sends))
+        pl.when(corner_west)(functools.partial(start, corner_west_sends))
+        pl.when(corner_east)(functools.partial(start, corner_east_sends))
+
+    @pl.when(origin)
+    def _():
+        pl.semaphore_wait(barrier, even_count)
+        for target in ((1, 0), (1, 1), (1, lons - 1)):
+            greet(target)
+
+    @pl.when(jnp.logical_and(upper, even))
+    def _():
+        pl.semaphore_wait(barrier, even_count)
+        tell(0)
+
+    @pl.when(jnp.logical_and(no(upper), no(even)))
+    def _():
+        pl.semaphore_wait(barrier, odd_count)
+        pl.when(jnp.logical_or(origin_mate, beside_desk))(functools.partial(greet, root))
+        pl.when(no(origin_mate))(functools.partial(tell, 0))
+
+    @pl.when(upper == (odd == 1))
+    def _():
+        pl.semaphore_wait(told.at[0], 1)
+
+    pl.when(both(upper, has_far))(functools.partial(start, far_sends[2:6] + far_sends[:1]))
+    pl.when(no(upper))(start_sides)
+    pl.when(no(origin_mate))(functools.partial(start, mate_sends))
+
+    @pl.when(origin_mate)
+    def _():
+        pl.semaphore_wait(barrier, 1)
+        tell(0)
+        start(mate_sends)
 
     @pl.when(jnp.logical_not(has_far))
     def _():
@@ -234,6 +293,38 @@
         reverse(row)
         forward_matrix(row)
         backward_blocks(row)
+
+    @pl.when(both(no(upper), even))
+    def _():
+        pl.when(no(origin))(lambda: pl.semaphore_wait(barrier, even_count))
+        tell(1)
+
+    @pl.when(both(upper, no(even)))
+    def _():
+        pl.semaphore_wait(barrier, odd_count)
+        tell(1)
+
+    @pl.when(upper == even)
+    def _():
+        pl.semaphore_wait(told.at[1], 1)
+
+    pl.when(both(no(upper), has_far))(
+        functools.partial(start, far_sends[2:6] + far_sends[:2] + far_sends[6:])
+    )
+
+    pl.when(upper)(start_sides)
+    pl.when(both(upper, has_far))(functools.partial(start, far_sends[1:2] + far_sends[6:]))
+
+    @pl.when(beside_desk)
+    def _():
+        pl.semaphore_wait(barrier, 1)
+        tell(2)
+
+    @pl.when(beside_even)
+    def _():
+        pl.semaphore_wait(told.at[2], 1)
+        pl.when(lon == 1)(functools.partial(start, west_sends))
+        pl.when(lon == lons - 1)(functools.partial(start, east_sends))
 
     for load in loads[4:]:
         load.wait()
@@ -299,6 +390,7 @@
 
     for copy in lon_sends:
         copy.wait_recv()
+    pl.when(no(origin))(functools.partial(start, corner_sends))
     for row in range(ROWS):
         fill_cells(row, own[1 + row], w_in[row], e_in[row])
         fill_cots(row, own[(0, 6, 7, 5)[row]], cw_in[row], ce_in[row])
@@ -336,9 +428,15 @@
     advance((ROWS - 1, ROWS), ready=(2, 1))
     result_ref[...] = wide[...].astype(BF16)
 
-    for copies in groups:
+    def drain(copies):
         for copy in copies:
             copy.wait_send()
+
+    for copies in groups:
+        drain(copies)
+    pl.when(no(origin))(functools.partial(drain, corner_sends))
+    pl.when(corner_west)(functools.partial(drain, corner_west_sends))
+    pl.when(corner_east)(functools.partial(drain, corner_east_sends))
 
     @pl.when(has_far)
     def _():
@@ -438,8 +536,9 @@
             held(chans, HID),
             held(HID, chans),
             pltpu.SemaphoreType.DMA((7,)),
-            pltpu.SemaphoreType.DMA((16,)),
-            pltpu.SemaphoreType.DMA((16,)),
+            pltpu.SemaphoreType.DMA((21,)),
+            pltpu.SemaphoreType.DMA((17,)),
+            pltpu.SemaphoreType.REGULAR((3,)),
         ],
         compiler_params=pltpu.CompilerParams(
             collective_id=0, has_side_effects=True, vmem_limit_bytes=24 << 20

time: 26.2 us -> 25.4 us (0.969)
  Pallas kernels: 25.4 us -> 24.6 us
    pallas_call x1, Pallas kernels: 24 us -> 23.2 us  [on_device(): pl.pallas_call(functools.partial(forward_kernel, width), name='halo_forwa...]
where the time goes in v3:
time: 25.4 us; the launch traced here: 25.3 us
  Pallas kernels  24.6 us (97%)
  between operations  0.64 us (3%)
    pallas_call x1, Pallas kernels, on_device(): pl.pallas_call(functools.partial(forward_kernel, width), name='halo_forwa...  23.2 us
    pallas_call x1, Pallas kernels, on_device(): pl.pallas_call(functools.partial(backward_kernel, width), name='transpose...  1.43 us

profile of v3, /device:TPU:513, one launch (start us, length us, event | category | flops | bytes accessed | tf_op | source)
XLA Modules:
  0.0 25.3 jit_solution(15043353171257154606)
XLA Ops:
  0.6 23.2 %halo_forward.1 = (bf16[720,128]{1,0:T(8,128)(2,1)S(1)}, bf16[6,128,256]{2,1,0:T(8,128)(2,1)S(1)}, bf16[4,384,384]{2,1,0:T(8,128)(2,1)S(1)}, bf16[256,1024]{1,0:T(8,128)(2,1)S(1)}, f32[192,256]{1,0:T(8,128)S(1)}) custom-call(bf16[720,128]{1,0:T(8,128)(2,1)} %bitcast.31, bf16[720,128]{1,0:T(8,128)(2,1)} %bitcast.32, bf16[256,1024]{1,0:T(8,128)(2,1)} %w_mix_hbm.1, ...), custom_call_target="tpu_custom_call" | custom-call | tf_op jit(solution)/shard_map/halo_forward/pallas_call | solution.py:490
  23.9 1.4 %transposed_mix.1 = (bf16[720,128]{1,0:T(8,128)(2,1)}, bf16[720,128]{1,0:T(8,128)(2,1)}) custom-call(bf16[720,128]{1,0:T(8,128)(2,1)S(1)} %get-tuple-element.9.packed_result, bf16[6,128,256]{2,1,0:T(8,128)(2,1)S(1)} %get-tuple-element.10.grads_ref, bf16[4,384,384]{2,1,0:T(8,128)(2,1)S(1)} %get-tuple-element.11.back_ref, ...), custom_call_target="tpu_custom_call" | custom-call | tf_op jit(solution)/shard_map/transposed_mix/pallas_call | solution.py:547

commit v4 on v3

--- a/solution.py
+++ b/solution.py
@@ -289,42 +289,42 @@
                     circulant(line, OUTC, 0).astype(BF16)
                 )
 
+    @pl.when(both(no(upper), even))
+    def _():
+        pl.when(no(origin))(lambda: pl.semaphore_wait(barrier, even_count))
+        tell(1)
+
+    @pl.when(both(upper, no(even)))
+    def _():
+        pl.semaphore_wait(barrier, odd_count)
+        tell(1)
+
+    @pl.when(upper == even)
+    def _():
+        pl.semaphore_wait(told.at[1], 1)
+
+    pl.when(both(no(upper), has_far))(
+        functools.partial(start, far_sends[2:6] + far_sends[:2] + far_sends[6:])
+    )
+
+    pl.when(upper)(start_sides)
+    pl.when(both(upper, has_far))(functools.partial(start, far_sends[1:2] + far_sends[6:]))
+
+    @pl.when(beside_desk)
+    def _():
+        pl.semaphore_wait(barrier, 1)
+        tell(2)
+
+    @pl.when(beside_even)
+    def _():
+        pl.semaphore_wait(told.at[2], 1)
+        pl.when(lon == 1)(functools.partial(start, west_sends))
+        pl.when(lon == lons - 1)(functools.partial(start, east_sends))
+
     for row in range(ROWS):
         reverse(row)
         forward_matrix(row)
         backward_blocks(row)
-
-    @pl.when(both(no(upper), even))
-    def _():
-        pl.when(no(origin))(lambda: pl.semaphore_wait(barrier, even_count))
-        tell(1)
-
-    @pl.when(both(upper, no(even)))
-    def _():
-        pl.semaphore_wait(barrier, odd_count)
-        tell(1)
-
-    @pl.when(upper == even)
-    def _():
-        pl.semaphore_wait(told.at[1], 1)
-
-    pl.when(both(no(upper), has_far))(
-        functools.partial(start, far_sends[2:6] + far_sends[:2] + far_sends[6:])
-    )
-
-    pl.when(upper)(start_sides)
-    pl.when(both(upper, has_far))(functools.partial(start, far_sends[1:2] + far_sends[6:]))
-
-    @pl.when(beside_desk)
-    def _():
-        pl.semaphore_wait(barrier, 1)
-        tell(2)
-
-    @pl.when(beside_even)
-    def _():
-        pl.semaphore_wait(told.at[2], 1)
-        pl.when(lon == 1)(functools.partial(start, west_sends))
-        pl.when(lon == lons - 1)(functools.partial(start, east_sends))
 
     for load in loads[4:]:
         load.wait()
@@ -347,7 +347,7 @@
         source = cells[row + 1 + begin : row + 1 + end].reshape((end - begin) * RING, CH)
         return dot(fwd[row + 1, :, begin * RING : end * RING], source)
 
-    def advance(rows, ready=None):
+    def advance(rows, ready=None, between=None):
         count = len(rows)
         convs = []
         for n, row in enumerate(rows):
@@ -370,20 +370,24 @@
         pre = dot(hidden, w_up[...])
         half = 0.5 * (1.0 + lax.erf(pre * 0.7071067811865476))
         slope = half + pre * jnp.exp(-0.5 * pre * pre) * 0.3989422804014327
+        active = (half * pre).astype(BF16)
+        for n, row in enumerate(rows):
+            base = n * CELLS
+            if 0 <= row < ROWS:
+                result = hidden[base : base + OUTC].astype(F32) + dot(
+                    active[base : base + OUTC], w_down[...]
+                )
+                write_row(wide, owned(odd, row), width, result[:width])
+        if between is not None:
+            between()
         upstream = jnp.concatenate([cots[row + 1] for row in rows], axis=0)
         grad_active = (dot_last(upstream, w_down[...]) * slope).astype(BF16)
         grad = (upstream.astype(F32) + dot_last(grad_active, w_up[...])).astype(BF16)
-        active = (half * pre).astype(BF16)
         for n, row in enumerate(rows):
             base = n * CELLS
             grads_ref[row + 1, 0:104] = grad[base : base + 104]
             grads_ref[row + 1, 104:120] = jnp.zeros((WIDE, CH), BF16)
             grads_ref[row + 1, 120:128] = grad[base + 104 : base + CELLS]
-            if 0 <= row < ROWS:
-                result = hidden[base : base + OUTC].astype(F32) + dot(
-                    active[base : base + OUTC], w_down[...]
-                )
-                write_row(wide, owned(odd, row), width, result[:width])
 
     def finish(rows):
         return retreat(rows, grads_ref, back_ref, w_mix)
@@ -419,14 +423,18 @@
 
     @pl.when(has_far)
     def _():
-        for copy in far_sends[1:]:
+        for copy in far_sends[1:6]:
             copy.wait_recv()
 
     fill_cells(ROWS, far_in[1], fw_in[1], fe_in[1])
     fill_cells(ROWS + 1, far_in[0], fw_in[0], fe_in[0])
-    fill_cots(ROWS, far_in[2], fcw_in[...], fce_in[...])
-    advance((ROWS - 1, ROWS), ready=(2, 1))
-    result_ref[...] = wide[...].astype(BF16)
+
+    def last_cots():
+        result_ref[...] = wide[...].astype(BF16)
+        pl.when(has_far)(far_sends[6].wait_recv)
+        fill_cots(ROWS, far_in[2], fcw_in[...], fce_in[...])
+
+    advance((ROWS - 1, ROWS), ready=(2, 1), between=last_cots)
 
     def drain(copies):
         for copy in copies:

time: 25.4 us -> 24.6 us (0.969)
  the two profiles are of different devices: /device:TPU:513 before, /device:TPU:385 now
where the time goes in v4:
time: 24.6 us; the launch traced here: 24.4 us
  Pallas kernels  23.8 us (97%)
  between operations  0.64 us (3%)
    pallas_call x1, Pallas kernels, on_device(): pl.pallas_call(functools.partial(forward_kernel, width), name='halo_forwa...  22.4 us
    pallas_call x1, Pallas kernels, on_device(): pl.pallas_call(functools.partial(backward_kernel, width), name='transpose...  1.43 us

profile of v4, /device:TPU:385, one launch (start us, length us, event | category | flops | bytes accessed | tf_op | source)
XLA Modules:
  0.0 24.4 jit_solution(12326728168711536342)
XLA Ops:
  0.6 22.4 %halo_forward.1 = (bf16[720,128]{1,0:T(8,128)(2,1)S(1)}, bf16[6,128,256]{2,1,0:T(8,128)(2,1)S(1)}, bf16[4,384,384]{2,1,0:T(8,128)(2,1)S(1)}, bf16[256,1024]{1,0:T(8,128)(2,1)S(1)}, f32[192,256]{1,0:T(8,128)S(1)}) custom-call(bf16[720,128]{1,0:T(8,128)(2,1)} %bitcast.31, bf16[720,128]{1,0:T(8,128)(2,1)} %bitcast.32, bf16[256,1024]{1,0:T(8,128)(2,1)} %w_mix_hbm.1, ...), custom_call_target="tpu_custom_call" | custom-call | tf_op jit(solution)/shard_map/halo_forward/pallas_call | solution.py:498
  23.0 1.4 %transposed_mix.1 = (bf16[720,128]{1,0:T(8,128)(2,1)}, bf16[720,128]{1,0:T(8,128)(2,1)}) custom-call(bf16[720,128]{1,0:T(8,128)(2,1)S(1)} %get-tuple-element.9.packed_result, bf16[6,128,256]{2,1,0:T(8,128)(2,1)S(1)} %get-tuple-element.10.grads_ref, bf16[4,384,384]{2,1,0:T(8,128)(2,1)S(1)} %get-tuple-element.11.back_ref, ...), custom_call_target="tpu_custom_call" | custom-call | tf_op jit(solution)/shard_map/transposed_mix/pallas_call | solution.py:555

commit v5 on v4

--- a/solution.py
+++ b/solution.py
@@ -143,14 +143,14 @@
 
     for load, source, slots in ((loads[0], raw, (1, 2, 3, 4)), (loads[1], raw_cot, (0, 6, 7, 5))):
         load.wait()
-        wide[...] = source[...].astype(F32)
+        wide[0 : source.shape[0]] = source[...].astype(F32)
         for row in range(ROWS):
             own[slots[row]] = read_row(wide, owned(odd, row), width).astype(BF16)
 
     loads[2].wait()
     loads[3].wait()
     taps[...] = jnp.zeros_like(taps)
-    filters_wide[...] = filters_ref[...].astype(F32)
+    filters_wide[0 : 3 * KB * ROWS] = filters_ref[...].astype(F32)
     lane = lax.broadcasted_iota(jnp.int32, (1, TAPS), 1) - REACH
     for row in range(ROWS):
         keep = jnp.abs(lane) <= reach_ref[owned(odd, row)]
@@ -430,7 +430,7 @@
     fill_cells(ROWS + 1, far_in[0], fw_in[0], fe_in[0])
 
     def last_cots():
-        result_ref[...] = wide[...].astype(BF16)
+        result_ref[...] = wide[0 : result_ref.shape[0]].astype(BF16)
         pl.when(has_far)(far_sends[6].wait_recv)
         fill_cots(ROWS, far_in[2], fcw_in[...], fce_in[...])
 
@@ -474,7 +474,7 @@
     for row in (0, 1):
         write_row(wide, owned(odd, row), width, done_ref[row * OUTC : row * OUTC + width])
         write_row(wide, owned(odd, 2 + row), width, total[row * OUTC : row * OUTC + width])
-    out[...] = wide[...].astype(BF16)
+    out[...] = wide[0 : out.shape[0]].astype(BF16)
     store_grad = pltpu.make_async_copy(out, grad_hbm, sems.at[1])
     store_grad.start()
     store_result.wait()
@@ -486,6 +486,7 @@
     hbm = pl.BlockSpec(memory_space=pltpu.HBM)
     vmem = pl.BlockSpec(memory_space=pltpu.VMEM)
     tiles = (width * rows * chans // LANES, LANES)
+    roomy = (-(-width // 8) * 8 * rows * chans // LANES, LANES)
 
     def held(*shape, kind=BF16):
         return pltpu.VMEM(shape, kind)
@@ -510,9 +511,9 @@
         scratch_shapes=[
             held(*tiles),
             held(*tiles),
-            held(*tiles, kind=F32),
+            held(*roomy, kind=F32),
             held(3 * KB * rows, TAPS),
-            held(3 * KB * rows, TAPS, kind=F32),
+            held(4 * KB * rows, TAPS, kind=F32),
             pltpu.SMEM((rows,), jnp.int32),
             held(8, width, chans),
             held(rows, WIDE, chans),
@@ -559,7 +560,7 @@
         in_specs=[vmem] * 5,
         out_specs=(hbm, hbm),
         scratch_shapes=[
-            held(*tiles, kind=F32),
+            held(*roomy, kind=F32),
             held(*tiles),
             pltpu.SemaphoreType.DMA((2,)),
         ],

time: 24.6 us -> 24.6 us (level)
  no operation moved by 1% of the time
where the time goes in v5:
time: 24.6 us; the launch traced here: 24.4 us
  Pallas kernels  23.8 us (97%)
  between operations  0.64 us (3%)
    pallas_call x1, Pallas kernels, on_device(): pl.pallas_call(functools.partial(forward_kernel, width), name='halo_forwa...  22.4 us
    pallas_call x1, Pallas kernels, on_device(): pl.pallas_call(functools.partial(backward_kernel, width), name='transpose...  1.43 us

profile of v5, /device:TPU:385, one launch (start us, length us, event | category | flops | bytes accessed | tf_op | source)
XLA Modules:
  0.0 24.4 jit_solution(11624905061604024937)
XLA Ops:
  0.6 22.4 %halo_forward.1 = (bf16[720,128]{1,0:T(8,128)(2,1)S(1)}, bf16[6,128,256]{2,1,0:T(8,128)(2,1)S(1)}, bf16[4,384,384]{2,1,0:T(8,128)(2,1)S(1)}, bf16[256,1024]{1,0:T(8,128)(2,1)S(1)}, f32[192,256]{1,0:T(8,128)S(1)}) custom-call(bf16[720,128]{1,0:T(8,128)(2,1)} %bitcast.31, bf16[720,128]{1,0:T(8,128)(2,1)} %bitcast.32, bf16[256,1024]{1,0:T(8,128)(2,1)} %w_mix_hbm.1, ...), custom_call_target="tpu_custom_call" | custom-call | tf_op jit(solution)/shard_map/halo_forward/pallas_call | solution.py:499
  23.0 1.4 %transposed_mix.1 = (bf16[720,128]{1,0:T(8,128)(2,1)}, bf16[720,128]{1,0:T(8,128)(2,1)}) custom-call(bf16[720,128]{1,0:T(8,128)(2,1)S(1)} %get-tuple-element.9.packed_result, bf16[6,128,256]{2,1,0:T(8,128)(2,1)S(1)} %get-tuple-element.10.grads_ref, bf16[4,384,384]{2,1,0:T(8,128)(2,1)S(1)} %get-tuple-element.11.back_ref, ...), custom_call_target="tpu_custom_call" | custom-call | tf_op jit(solution)/shard_map/transposed_mix/pallas_call | solution.py:556

commit v6 on v5

--- a/solution.py
+++ b/solution.py
@@ -79,7 +79,7 @@
 def forward_kernel(
     width,
     fields_hbm, cot_hbm, w_mix_hbm, w_up_hbm, w_down_hbm, filters_hbm, reach_hbm,
-    result_ref, grads_ref, back_ref, w_mix, done_ref,
+    result_ref, grads_ref, back_ref, w_mix, done_ref, begun_ref,
     raw, raw_cot, wide, filters_ref, filters_wide, reach_ref,
     own, edge, cot_w, cot_e, taps_own, near_in, far_in, taps_near, taps_far,
     w_in, e_in, cw_in, ce_in, nw_in, ne_in, ncw_in, nce_in, fw_in, fe_in, fcw_in, fce_in,
@@ -418,6 +418,8 @@
     reverse(ROWS)
     forward_matrix(ROWS)
     backward_blocks(ROWS)
+    begun_ref[0] = back_part(2, 0, 2, grads_ref, back_ref)
+    begun_ref[1] = back_part(3, 0, 1, grads_ref, back_ref)
     partial_ref[0] = conv_part(ROWS - 1, 0, 2)
     partial_ref[1] = conv_part(ROWS, 0, 1)
 
@@ -452,11 +454,19 @@
             copy.wait_send()
 
 
-def retreat(rows, grads_ref, back_ref, w_mix):
+def back_part(row, begin, end, grads_ref, back_ref):
+    source = grads_ref[row + begin : row + end].reshape((end - begin) * RING, CH)
+    return dot(back_ref[row, :, begin * RING : end * RING], source)
+
+
+def retreat(rows, grads_ref, back_ref, w_mix, begun=None):
     convs = []
-    for row in rows:
-        source = grads_ref[row : row + 3].reshape(3 * RING, CH)
-        convs.append(dot(back_ref[row], source).astype(BF16))
+    for n, row in enumerate(rows):
+        if begun is None:
+            conv = back_part(row, 0, 3, grads_ref, back_ref)
+        else:
+            conv = begun[n] + back_part(row, 2 - n, 3, grads_ref, back_ref)
+        convs.append(conv.astype(BF16))
     total = jnp.concatenate([grads_ref[row + 1, 0:OUTC].astype(F32) for row in rows], axis=0)
     for basis in range(KB):
         part = jnp.concatenate([c[basis * OUTC : (basis + 1) * OUTC] for c in convs], axis=0)
@@ -465,12 +475,12 @@
 
 
 def backward_kernel(
-    width, packed_result, grads_ref, back_ref, w_mix, done_ref, result_hbm, grad_hbm, wide, out, sems
+    width, packed_result, grads_ref, back_ref, w_mix, done_ref, begun_ref, result_hbm, grad_hbm, wide, out, sems
 ):
     odd = lax.rem(lax.axis_index("lat"), 2)
     store_result = pltpu.make_async_copy(packed_result, result_hbm, sems.at[0])
     store_result.start()
-    total = retreat((2, 3), grads_ref, back_ref, w_mix)
+    total = retreat((2, 3), grads_ref, back_ref, w_mix, begun_ref)
     for row in (0, 1):
         write_row(wide, owned(odd, row), width, done_ref[row * OUTC : row * OUTC + width])
         write_row(wide, owned(odd, 2 + row), width, total[row * OUTC : row * OUTC + width])
@@ -496,7 +506,7 @@
         filters.transpose(0, 2, 1, 3).reshape(3 * KB * rows, TAPS), reach,
     )
     sources = [pltpu.with_memory_space_constraint(source, pltpu.HBM) for source in sources]
-    result, grads, back, held_mix, done = pl.pallas_call(
+    result, grads, back, held_mix, done, begun = pl.pallas_call(
         functools.partial(forward_kernel, width),
         name="halo_forward",
         out_shape=(
@@ -505,9 +515,10 @@
             held(rows, KB * OUTC, 3 * RING),
             held(chans, KB * chans),
             held(2 * OUTC, chans, kind=F32),
+            held(2, KB * OUTC, chans, kind=F32),
         ),
         in_specs=[hbm] * 7,
-        out_specs=(vmem,) * 5,
+        out_specs=(vmem,) * 6,
         scratch_shapes=[
             held(*tiles),
             held(*tiles),
@@ -557,7 +568,7 @@
         functools.partial(backward_kernel, width),
         name="transposed_mix",
         out_shape=(pltpu.HBM(tiles, BF16), pltpu.HBM(tiles, BF16)),
-        in_specs=[vmem] * 5,
+        in_specs=[vmem] * 6,
         out_specs=(hbm, hbm),
         scratch_shapes=[
             held(*roomy, kind=F32),
@@ -565,7 +576,7 @@
             pltpu.SemaphoreType.DMA((2,)),
         ],
         compiler_params=pltpu.CompilerParams(vmem_limit_bytes=16 << 20),
-    )(result, grads, back, held_mix, done)
+    )(result, grads, back, held_mix, done, begun)
     return unpacked(result, rows, width, chans), unpacked(field_grad, rows, width, chans)
 
 

time: 24.6 us -> 24.3 us (0.988)
  the two profiles are of different devices: /device:TPU:385 before, /device:TPU:520 now
where the time goes in v6:
time: 24.3 us; the launch traced here: 24.2 us
  Pallas kernels  23.6 us (97%)
  between operations  0.64 us (3%)
    pallas_call x1, Pallas kernels, on_device(): pl.pallas_call(functools.partial(forward_kernel, width), name='halo_forwa...  22.4 us
    pallas_call x1, Pallas kernels, on_device(): pl.pallas_call(functools.partial(backward_kernel, width), name='transpose...  1.17 us

profile of v6, /device:TPU:520, one launch (start us, length us, event | category | flops | bytes accessed | tf_op | source)
XLA Modules:
  0.0 24.2 jit_solution(7428867810152521321)
XLA Ops:
  0.6 22.4 %halo_forward.1 = (bf16[720,128]{1,0:T(8,128)(2,1)S(1)}, bf16[6,128,256]{2,1,0:T(8,128)(2,1)S(1)}, bf16[4,384,384]{2,1,0:T(8,128)(2,1)S(1)}, bf16[256,1024]{1,0:...) custom-call(bf16[720,128]{1,0:T(8,128)(2,1)} %bitcast.31, bf16[720,128]{1,0:T(8,128)(2,1)} %bitcast.32, ...), custom_call_target="tpu_custom_call" | custom-call | tf_op jit(solution)/shard_map/halo_forward/pallas_call | solution.py:509
  23.0 1.2 %transposed_mix.1 = (bf16[720,128]{1,0:T(8,128)(2,1)}, bf16[720,128]{1,0:T(8,128)(2,1)}) custom-call(bf16[720,128]{1,0:T(8,128)(2,1)S(1)} %get-tuple-element.10.packed_result, bf16[6,128,256]{2,1,0:T(8,128)(2,1)S(1)} %get-tuple-element.11.grads_ref, bf16[4,384,384]{2,1,0:T(8,128)(2,1)S(1)} %get-tuple-element.12.back_ref, ...), custom_call_target="tpu_custom_call" | custom-call | tf_op jit(solution)/shard_map/transposed_mix/pallas_call | solution.py:567
